TPU v7x, 128 devices: a whole 4x4x4 slice. The times are simulated.
128 devices in a mesh: grp: 8 (over y, core), tok: 16 (over z, x).
Axes of the slice: x: 4, y: 4, z: 4, core: 2. Of those that a mesh axis runs over, the one named last changes fastest.
Arguments:
- pre_q: bfloat16 [8192, 4096], P(('grp', 'tok')), may hold values from -64 to 64
- pre_kv: bfloat16 [8192, 2048], P(('grp', 'tok')), may hold values from -8 to 8
- pre_segment: int32 [8, 1024], P('grp'), may hold values from 0 to 3, never falling along the last dimension, each value on 1 to 512 neighbouring positions
- dec_q: bfloat16 [128, 4096], P(('grp', 'tok')), may hold values from -64 to 64
- cache: bfloat16 [128, 512, 2048], P(('grp', 'tok')), may hold values from -8 to 8
- cache_len: int32 [128], P(('grp', 'tok')), may hold values from 1 to 512, 32768 in all
- slot_request: int32 [128], replicated, may hold values from 0 to 127, each once
- resid: bfloat16 [8320, 4096], P('grp', 'tok'), may hold values from -64 to 64
- wo: bfloat16 [4096, 4096], P(None, 'tok'), may hold values from -0.5 to 0.5
- tenant: int32 [8, 1040], P('grp'), may hold values from 0 to 3, never falling along the last dimension, each value on 1 to 520 neighbouring positions
- norm_gain: float32 [4, 4096], replicated, may hold values from 0.25 to 1.75
- w_gate: bfloat16 [4096, 12288], P(None, 'tok'), may hold values from -0.09375 to 0.09375
- w_up: bfloat16 [4096, 12288], P(None, 'tok'), may hold values from -0.09375 to 0.09375
- w_down: bfloat16 [12288, 4096], P('tok'), may hold values from -0.0546875 to 0.0546875
Outputs:
- out: bfloat16 [8320, 4096], P('grp', 'tok')
All inputs are finite; a program needn't handle non-finite values. No bound on the sum of `cache_len` on one device may be relied on, other than what follows from the above.
Results may differ from a plain program's by a relative error of at most 0.011.
Values may be sent and summed in bfloat16 or wider, within the bound.
A program may use at most 128 MiB of HBM per device.

v0:
```python
import math

import jax
import jax.numpy as jnp
from jax import lax
from jax.sharding import PartitionSpec as P

D = 4096
H = 32
KVH = 8
HD = 128


epsilon = 1e-05


def laid_out(blocks, dim):
    dims = list(blocks.shape[1:])
    dims[dim] *= blocks.shape[0]
    return jnp.moveaxis(blocks, 0, dim).reshape(dims)


def piecewise(x, axis, dim, apply, out_dim):
    size, span = (lax.axis_size(axis), x.shape[dim])
    count = 2 if span % 2 == 0 else 1
    gathered, length = ([], span // count)
    for k in range(count):
        share = lax.slice_in_dim(x, k * length, (k + 1) * length, axis=dim)
        starts = jnp.arange(size) * span + k * length
        gathered.append(jax.vmap(apply)(lax.all_gather(share, axis), starts))
    return laid_out(jnp.concatenate(gathered, axis=out_dim + 1), out_dim)


def copy_for_each(x, axis):
    copies = jnp.broadcast_to(x, (lax.axis_size(axis), *x.shape))
    return lax.all_to_all(copies, axis, split_axis=0, concat_axis=0, tiled=True)


def over_copies(x, axis):
    return copy_for_each(x, axis).sum(axis=0)


def shards(
    pre_q,
    pre_kv,
    pre_segment,
    dec_q,
    cache,
    cache_len,
    slot_request,
    resid,
    wo,
    tenant,
    norm_gain,
    w_gate,
    w_up,
    w_down,
):
    group = H // KVH
    width = KVH * HD
    tok_index = lax.axis_index("tok")
    local_rows = pre_q.shape[0]
    segment = pre_segment[0]
    query_pos = tok_index * local_rows + jnp.arange(local_rows)
    query_seg = lax.dynamic_slice_in_dim(segment, tok_index * local_rows, local_rows)
    queries = pre_q.reshape(local_rows, KVH, group, HD)
    piece = lax.all_gather(pre_kv, "tok", axis=0, tiled=True)
    running = jnp.full((KVH, group, local_rows), -jnp.inf, jnp.float32)
    totals = jnp.zeros((KVH, group, local_rows), jnp.float32)
    summed = jnp.zeros((KVH, group, local_rows, HD), jnp.float32)
    count = piece.shape[0]
    keys = piece[:, :width].reshape(count, KVH, HD)
    values = piece[:, width:].reshape(count, KVH, HD)
    key_pos = jnp.arange(count)
    allowed = (key_pos[None, :] <= query_pos[:, None]) & (segment[None, :] == query_seg[:, None])
    scores = jnp.einsum(
        "qkgd,nkd->kgqn", queries, keys, preferred_element_type=jnp.float32
    ) / math.sqrt(HD)
    scores = jnp.where(allowed, scores, -jnp.inf)
    highest = jnp.max(scores, axis=-1)
    anchor = jnp.where(jnp.isfinite(highest), highest, 0.0)
    weights = jnp.exp(scores - anchor[..., None]).astype(jnp.bfloat16)
    factor = jnp.exp(running - anchor)
    totals = totals * factor + jnp.sum(weights.astype(jnp.float32), axis=-1)
    summed = summed * factor[..., None] + jnp.einsum(
        "kgqn,nkd->kgqd", weights, values, preferred_element_type=jnp.float32
    )
    running, totals, summed = (highest, totals, summed)
    prefill_out = (
        (summed / totals[..., None])
        .transpose(2, 0, 1, 3)
        .reshape(local_rows, D)
        .astype(jnp.bfloat16)
    )
    all_queries = lax.all_gather(dec_q, ("grp", "tok"), axis=0, tiled=True)
    slot = lax.axis_index(("grp", "tok"))
    request = slot_request[slot]
    query_row = lax.dynamic_slice_in_dim(all_queries, request, 1, 0).reshape(KVH, group, HD)
    positions = cache.shape[1]
    entries = cache[0].reshape(positions, 2, KVH, HD)
    slot_scores = jnp.einsum(
        "kgd,pkd->kgp", query_row, entries[:, 0], preferred_element_type=jnp.float32
    ) / math.sqrt(HD)
    visible = jnp.arange(positions) < cache_len[0]
    slot_scores = jnp.where(visible, slot_scores, -jnp.inf)
    slot_top = jnp.max(slot_scores, axis=-1, keepdims=True)
    slot_weights = jnp.exp(slot_scores - slot_top).astype(jnp.bfloat16)
    slot_total = jnp.sum(slot_weights.astype(jnp.float32), axis=-1)
    slot_mixed = jnp.einsum(
        "kgp,pkd->kgd", slot_weights, entries[:, 1], preferred_element_type=jnp.float32
    )
    decode_out = (slot_mixed / slot_total[..., None]).reshape(1, D).astype(jnp.bfloat16)
    attended = jnp.concatenate([prefill_out, decode_out], axis=0)

    def project(piece, start):
        return jnp.dot(piece, wo, preferred_element_type=jnp.float32)

    projected = piecewise(attended, "tok", 0, project, 0)
    mixed_in = (resid.astype(jnp.float32) + projected).astype(jnp.bfloat16)
    col_count = mixed_in.shape[1]
    owners = tenant[0]
    one_hot = (owners[:, None] == jnp.arange(norm_gain.shape[0])[None, :]).astype(jnp.float32)
    wide_cols = mixed_in.astype(jnp.float32)
    partial_sq = jnp.sum(wide_cols * wide_cols, axis=-1)
    square_sum = over_copies(partial_sq, "tok")
    local_gain = lax.dynamic_slice_in_dim(norm_gain, tok_index * col_count, col_count, 1)
    gains = jnp.dot(one_hot, local_gain, precision=lax.Precision.HIGHEST)
    normed_part = (wide_cols * lax.rsqrt(square_sum / D + epsilon)[:, None] * gains).astype(
        jnp.bfloat16
    )
    piece = lax.all_gather(normed_part, "tok", axis=1, tiled=True)
    gate_part = jnp.dot(piece, w_gate, preferred_element_type=jnp.float32)
    lift_part = jnp.dot(piece, w_up, preferred_element_type=jnp.float32)
    hidden = (jax.nn.silu(gate_part) * lift_part).astype(jnp.bfloat16)
    summed_cols = lax.psum_scatter(
        lax.dot_general(
            w_down, hidden, (((0,), (1,)), ((), ())), preferred_element_type=jnp.float32
        ).astype(jnp.bfloat16),
        "tok",
        scatter_dimension=0,
        tiled=True,
    ).astype(jnp.float32)
    result = mixed_in.astype(jnp.float32) + summed_cols.T
    return result.astype(jnp.bfloat16)


def solution(mesh):
    in_specs = (
        P(("grp", "tok"), None),
        P(("grp", "tok"), None),
        P("grp", None),
        P(("grp", "tok"), None),
        P(("grp", "tok"), None, None),
        P(("grp", "tok")),
        P(),
        P("grp", "tok"),
        P(None, "tok"),
        P("grp", None),
        P(),
        P(None, "tok"),
        P(None, "tok"),
        P("tok", None),
    )
    out_specs = P("grp", "tok")
    return jax.shard_map(shards, mesh=mesh, in_specs=in_specs, out_specs=out_specs, check_vma=False)
```

profile of v0, /device:TPU:0, one launch (start us, length us, event | category | flops | bytes accessed | tf_op | source)
XLA Modules:
  0.0 468.2 jit_solution(10560985726428544450)
XLA Ops:
  6.5 0.0 copy-start
  6.5 0.0 copy-start.4
  6.5 0.0 all-gather.12.cloned.1.call-start
  6.5 0.7 all-gather.12.cloned.1.call-update
  7.3 0.0 all-gather.8.cloned.1.call-start
  7.3 0.7 all-gather.8.cloned.1.call-update
  8.0 0.0 all-gather.14.cloned.1.call-start
  8.1 1.2 dynamic_slice.13
  11.3 1.4 reshape.65
  12.7 4.0 copy.48
  17.3 0.0 copy-done.4
  17.3 0.1 fusion.29
  17.4 0.1 fusion.22
  17.5 60.5 %all-gather.12.cloned.1.call-done = bf16[128,1,4096]{2,1,0:T(2,128)(2,1)} async-done(((bf16[1,1,4096]{2,1,0:T(2,128)(2,1)}), bf16[128,1,4096]{2,1,0:T(2,128)(2,1)}) %all-gather.12.cloned.1.call-update) | async-done | bytes 1048592 | tf_op jit(solution)/shard_map/all_gather | solution.py:95
  78.1 0.8 dynamic-slice_reduce_fusion
  78.8 1.6 convert_reduce_fusion.1
  80.5 1.6 fusion.16
  82.1 47.2 %all-gather.8.cloned.1.call-done = bf16[1024,2048]{1,0:T(8,128)(2,1)} async-done(((bf16[64,2048]{1,0:T(8,128)(2,1)}), bf16[1024,2048]{1,0:T(8,128)(2,1)}) %all-gather.8.cloned.1.call-update) | async-done | bytes 4194320 | tf_op jit(solution)/shard_map/all_gather | solution.py:67
  129.3 4.7 fusion.33
  134.0 3.9 copy.59
  138.0 3.9 copy.60
  141.9 3.2 fusion.1
  145.1 0.0 copy-start.2
  145.1 2.2 convert_reduce_fusion
  147.3 0.0 copy-done.2
  147.3 2.9 fusion.14
  150.2 0.4 copy.47
  150.6 0.4 convert_element_type.63
  151.0 0.9 maximum_bitcast_fusion
  151.9 0.0 all-gather.14.cloned.1.call-update
  151.9 75.6 %all-gather.14.cloned.1.call-done = bf16[16,65,4096]{2,1,0:T(8,128)(2,1)} async-done(((bf16[1,65,4096]{2,1,0:T(8,128)(2,1)}), bf16[16,65,4096]{2,1,0:T(8,128)(2,1)}) %all-gather.14.cloned.1.call-update) | async-done | bytes 8519696 | tf_op jit(solution)/shard_map/all_gather | solution.py:30
  227.5 0.0 copy-done
  227.5 5.2 %fusion.9 = f32[16,65,256]{2,1,0:T(8,128)S(1)} fusion(bf16[16,65,4096]{2,1,0:T(8,128)(2,1)} %all-gather.14.cloned.1.call-done, bf16[4096,256]{1,0:T(8,128)(2,1)S(1)} %copy-done), kind=kOutput, calls=%fused_computation.15 | convolution fusion | flops 2181038080 | bytes 11681792 | tf_op jit(solution)/shard_map/vmap()/dot_general | solution.py:116
  232.7 0.0 copy-start.3
  232.7 0.2 reshape.68
  232.9 1.3 fusion.17
  234.2 0.7 broadcast_in_dim.47
  234.8 5.3 %all-to-all-start = ((f32[16,1,1040]{2,1,0:T(1,128)}), f32[16,1,1040]{2,1,0:T(1,128)S(1)}, u32[]{:S(2)}, u32[]{:S(2)}) async-start(f32[16,1,1040]{2,1,0:T(1,128)} %broadcast_in_dim.47), calls=%async_computation | async-start | bytes 147456 | tf_op jit(solution)/shard_map/all_to_all | solution.py:36
  240.1 0.0 all-gather.10.cloned.1.call-start
  240.1 0.0 copy-done.3
  240.2 7.6 %all-to-all-done = f32[16,1,1040]{2,1,0:T(1,128)S(1)} async-done(((f32[16,1,1040]{2,1,0:T(1,128)}), f32[16,1,1040]{2,1,0:T(1,128)S(1)}, u32[]{:S(2)}, u32[]{:S(2)}) %all-to-all-start) | async-done | bytes 66592 | tf_op jit(solution)/shard_map/all_to_all | solution.py:36
  247.8 0.1 reduce_sum.42
  247.9 2.1 fusion.8
  250.0 0.0 all-gather.10.cloned.1.call-update
  250.0 0.2 reduce-scatter.2.cloned.1.call-start
  250.2 76.7 %all-gather.10.cloned.1.call-done = bf16[1040,4096]{1,0:T(8,128)(2,1)} async-done(((bf16[1040,256]{1,0:T(8,128)(2,1)}), bf16[1040,4096]{1,0:T(8,128)(2,1)}) %all-gather.10.cloned.1.call-update) | async-done | bytes 8519696 | tf_op jit(solution)/shard_map/all_gather | solution.py:131
  327.0 12.2 %fusion.34 = f32[1040,768]{1,0:T(8,128)} fusion(bf16[1040,4096]{1,0:T(8,128)(2,1)} %all-gather.10.cloned.1.call-done, bf16[4096,768]{1,0:T(8,128)(2,1)} %param.25), kind=kOutput, calls=%fused_computation.62 | convolution fusion | flops 6543114240 | bytes 18006016 | tf_op jit(solution)/shard_map/dot_general | solution.py:132
  339.2 26.3 %fusion = bf16[4096,1040]{0,1:T(8,128)(2,1)} fusion(bf16[768,4096]{1,0:T(8,128)(2,1)} %param.27, bf16[1040,4096]{1,0:T(8,128)(2,1)} %all-gather.10.cloned.1.call-done, bf16[4096,768]{1,0:T(8,128)(2,1)} %param.26, f32[1040,768]{1,0:T(8,128)} %fusion.34), kind=kOutput, calls=%fused_computation.1 | convolution fusion | flops 13095280640 | bytes 32817152 | tf_op jit(solution)/shard_map/dot_general | solution.py:136
  365.5 0.0 copy-start.1
  365.5 0.0 reduce-scatter.2.cloned.1.call-update
  365.5 94.2 %reduce-scatter.2.cloned.1.call-done = bf16[256,1040]{0,1:T(8,128)(2,1)} async-done(((bf16[4096,1040]{0,1:T(8,128)(2,1)}), bf16[256,1040]{0,1:T(8,128)(2,1)}) %reduce-scatter.2.cloned.1.call-update) | async-done | bytes 532496 | tf_op jit(solution)/shard_map/reduce_scatter | solution.py:135
  459.7 2.0 fusion.18
  461.7 0.0 copy-done.1
  (7 shorter events, 0.1 us)
Async XLA Ops:
  6.5 220.9 %copy-start = (bf16[4096,256]{1,0:T(8,128)(2,1)S(1)}, bf16[4096,256]{1,0:T(8,128)(2,1)}, u32[]{:S(2)}) copy-start(bf16[4096,256]{1,0:T(8,128)(2,1)} %param.22) | copy-start | bytes 6291460
  6.5 10.8 %copy-start.4 = (s32[1,1024]{1,0:T(1,128)S(1)}, s32[1,1024]{1,0:T(1,128)}, u32[]{:S(2)}) copy-start(s32[1,1024]{1,0:T(1,128)} %param.16) | copy-start | bytes 12292
  6.5 71.5 %all-gather.12.cloned.1.call-start = ((), (), s32[]{:S(2)}) async-start(), calls=%async_computation.5 | async-start | bytes 2113536 | tf_op jit(solution)/shard_map/all_gather | solution.py:95
  7.3 122.1 %all-gather.8.cloned.1.call-start = ((), (), s32[]{:S(2)}) async-start(), calls=%async_computation.2 | async-start | bytes 4456448 | tf_op jit(solution)/shard_map/all_gather | solution.py:67
  8.0 219.5 %all-gather.14.cloned.1.call-start = ((), (), s32[]{:S(2)}) async-start(), calls=%async_computation.6 | async-start | bytes 10027008 | tf_op jit(solution)/shard_map/all_gather | solution.py:30
  145.1 2.2 copy-start.2
  232.7 7.5 %copy-start.3 = (s32[1,1040]{1,0:T(1,128)S(1)}, s32[1,1040]{1,0:T(1,128)}, u32[]{:S(2)}) copy-start(s32[1,1040]{1,0:T(1,128)} %param.23) | copy-start | bytes 12484
  234.8 12.9 %all-to-all-start = ((f32[16,1,1040]{2,1,0:T(1,128)}), f32[16,1,1040]{2,1,0:T(1,128)S(1)}, u32[]{:S(2)}, u32[]{:S(2)}) async-start(f32[16,1,1040]{2,1,0:T(1,128)} %broadcast_in_dim.47), calls=%async_computation | async-start | bytes 147456 | tf_op jit(solution)/shard_map/all_to_all | solution.py:36
  240.1 86.9 %all-gather.10.cloned.1.call-start = ((), (), s32[]{:S(2)}) async-start(), calls=%async_computation.3 | async-start | bytes 9052160 | tf_op jit(solution)/shard_map/all_gather | solution.py:131
  250.0 209.7 %reduce-scatter.2.cloned.1.call-start = ((), (), s32[]{:S(2)}) async-start(), calls=%async_computation.4 | async-start | bytes 9052160 | tf_op jit(solution)/shard_map/reduce_scatter | solution.py:135
  365.5 96.2 %copy-start.1 = (bf16[4096,256]{1,0:T(8,128)(2,1)S(1)}, bf16[4096,256]{1,0:T(8,128)(2,1)}, u32[]{:S(2)}) copy-start(bf16[4096,256]{1,0:T(8,128)(2,1)} %param.22) | copy-start | bytes 6291460
Sparse Core Ops, SparseCore 0:
  10.3 67.6 all-gather.11
  80.2 49.1 all-gather.7
  152.0 75.4 all-gather.13
  250.1 76.8 all-gather.9
  365.7 93.9 reduce-scatter.1
where the time goes:
time: 469 us; the launch traced here: 468 us
  waiting for transfers between devices  363 us (77%)
  matrix products  55.2 us (12%)
  local copies, waits for them, and re-layouts  21.7 us (5%)
  between operations  15.9 us (3%)
  other arithmetic  6.54 us (1%)
  starting transfers between devices  5.6 us (1%)
    reduce_scatter x1, waiting for transfers between devices, shards(): lax.psum_scatter(lax.dot_general(w_down, hidden, (((0,), (1,)), ((), ()))...  94.2 us
    all_gather x1, waiting for transfers between devices, shards(): piece = lax.all_gather(normed_part, 'tok', axis=1, tiled=True)  76.7 us
    all_gather x1, waiting for transfers between devices, piecewise(): gathered.append(jax.vmap(apply)(lax.all_gather(share, axis), starts))  75.6 us
    all_gather x1, waiting for transfers between devices, shards(): all_queries = lax.all_gather(dec_q, ('grp', 'tok'), axis=0, tiled=True)  60.5 us
    all_gather x1, waiting for transfers between devices, shards(): piece = lax.all_gather(pre_kv, 'tok', axis=0, tiled=True)  47.2 us
    dot_general x1, matrix products, shards(): lax.dot_general(w_down, hidden, (((0,), (1,)), ((), ())), preferred_eleme...  26.3 us
    dot_general x1, matrix products, shards(): gate_part = jnp.dot(piece, w_gate, preferred_element_type=jnp.float32)  12.2 us
    unnamed x13, local copies, waits for them, and re-layouts  11.9 us
  transfers between devices with their start and end apart: 6, of which 6 were waited for; matrix products, arithmetic and copies ran while one was open for 2% of the time, Pallas kernels for 0%

commit v1 on v0

v1 whole, which is shorter than its diff:
```python
import functools
import math

import jax
import jax.numpy as jnp
from jax import lax
from jax.experimental import pallas as pl
from jax.experimental.pallas import tpu as pltpu
from jax.sharding import PartitionSpec as P

D = 4096
H = 32
KVH = 8
HD = 128
SIDE = 4
PEERS = SIDE * SIDE
BLOCK = D // PEERS
HALF = BLOCK // 2
WIDE = D // 2
SUB = 16
SPLIT = 112
CHUNKS = 5

epsilon = 1e-05
MESH = pl.DeviceIdType.MESH


def ring_kernel(
    att_ref,
    dec_ref,
    resid_ref,
    tenant_ref,
    gain_ref,
    wo_hbm,
    wg_hbm,
    wu_hbm,
    wd_hbm,
    out_ref,
    abuf,
    dbuf,
    xbuf,
    pbuf,
    mixed,
    normed,
    hidden,
    r1,
    r2,
    r3,
    r4,
    wo_ref,
    wg_ref,
    wu_ref,
    wd_ref,
    w_sem,
    a_send,
    a_recv,
    d_send,
    d_recv,
    x_send,
    x_recv,
    p_send,
    p_recv,
):
    me = lax.axis_index("tok")
    z, x = me // SIDE, me % SIDE
    rows = resid_ref.shape[0] // CHUNKS
    tiles = rows // SUB
    att_chunks = att_ref.shape[0] // SUB
    ffw = wg_ref.shape[1]
    parts = ((0, SPLIT), (SPLIT, rows - SPLIT))

    def hop(value, step):
        return lax.rem(value + step + SIDE, SIDE)

    def neighbour(axis, step):
        if axis == 0:
            return z * SIDE + hop(x, step)
        return hop(z, step) * SIDE + x

    def send(src, dst, sends, recvs, chunk, index, peer):
        return pltpu.make_async_remote_copy(
            src_ref=src,
            dst_ref=dst,
            send_sem=sends.at[chunk, index],
            recv_sem=recvs.at[chunk, index],
            device_id={"tok": peer},
            device_id_type=MESH,
        )

    def slot(level, half, way):
        return level * 4 + half * 2 + way

    steps = (1, -1)

    def row_span(chunk, part=None):
        base = chunk * rows
        if part is None:
            return pl.ds(pl.multiple_of(base, SUB), rows)
        return pl.ds(pl.multiple_of(base + parts[part][0], SUB), parts[part][1])

    def lanes(base, size):
        return pl.ds(pl.multiple_of(base, HALF), size)

    def near_lanes(half, offset):
        if half == 0:
            return lanes(z * 4 * HALF + hop(x, offset) * HALF, HALF)
        return lanes(WIDE + x * 4 * HALF + hop(z, offset) * HALF, HALF)

    def far_lanes(half, offset):
        if half == 0:
            return lanes(hop(z, offset) * 4 * HALF, 4 * HALF)
        return lanes(WIDE + hop(x, offset) * 4 * HALF, 4 * HALF)

    def a_cols(half, part):
        if part is None:
            return pl.ds(half * WIDE, WIDE)
        return pl.ds(half * WIDE + part * (WIDE // 2), WIDE // 2)

    def a_near(chunk, half, offset, part=None):
        if half == 0:
            return abuf.at[chunk * SIDE + z, hop(x, offset), :, a_cols(half, part)]
        return abuf.at[chunk * SIDE + hop(z, offset), x, :, a_cols(half, part)]

    def a_far(chunk, half, offset, part=None):
        if half == 0:
            return abuf.at[chunk * SIDE + hop(z, offset), :, :, a_cols(half, part)]
        return abuf.at[pl.ds(chunk * SIDE, SIDE), hop(x, offset), :, a_cols(half, part)]

    def x_near(chunk, half, offset, part=None):
        return xbuf.at[row_span(chunk, part), near_lanes(half, offset)]

    def x_far(chunk, half, offset, part=None):
        return xbuf.at[row_span(chunk, part), far_lanes(half, offset)]

    def gather_copy(near, far, sends, recvs, chunk, level, half, way, arriving):
        step = steps[way]
        axis = half if level < 2 else 1 - half
        block = near if level < 2 else far
        if level % 2 == 0:
            ref = block(chunk, half, -step if arriving else 0)
        else:
            ref = block(chunk, half, -2 * step if arriving else -step, way)
        return send(ref, ref, sends, recvs, chunk, slot(level, half, way), neighbour(axis, step))

    def gather_start(near, far, sends, recvs, chunk, level):
        for half in (0, 1):
            for way in (0, 1):
                gather_copy(near, far, sends, recvs, chunk, level, half, way, False).start()

    def gather_wait(near, far, sends, recvs, chunk, level):
        for half in (0, 1):
            for way in (0, 1):
                gather_copy(near, far, sends, recvs, chunk, level, half, way, True).wait_recv()

    def gather_sent(near, far, sends, recvs, chunk, level):
        for half in (0, 1):
            for way in (0, 1):
                gather_copy(near, far, sends, recvs, chunk, level, half, way, False).wait_send()

    a_args = (a_near, a_far, a_send, a_recv)
    x_args = (x_near, x_far, x_send, x_recv)

    def gather_step(args, chunk, level):
        gather_wait(*args, chunk, level)
        if level < 3:
            gather_start(*args, chunk, level + 1)

    def part_rows(part):
        return pl.ds(parts[part][0], parts[part][1])

    def scatter_copy(chunk, level, half, way):
        step = steps[way]
        axis = 1 - half if level < 2 else half
        if level == 0:
            src = pbuf.at[row_span(chunk, way), far_lanes(half, 2)]
            dst = r1.at[chunk, half, part_rows(way), :]
        elif level == 1:
            src = pbuf.at[row_span(chunk), far_lanes(half, step)]
            dst = r2.at[chunk, half, way]
        elif level == 2:
            src = pbuf.at[row_span(chunk, way), near_lanes(half, 2)]
            dst = r3.at[chunk, half, part_rows(way), :]
        else:
            src = pbuf.at[row_span(chunk), near_lanes(half, step)]
            dst = r4.at[chunk, half, way]
        return send(src, dst, p_send, p_recv, chunk, slot(level, half, way), neighbour(axis, step))

    def scatter_start(chunk, level):
        for half in (0, 1):
            for way in (0, 1):
                scatter_copy(chunk, level, half, way).start()

    def wide(value):
        return value.astype(jnp.float32)

    def scatter_step(chunk, level):
        for half in (0, 1):
            for way in (0, 1):
                scatter_copy(chunk, level, half, way).wait_recv()
            if level % 2 == 0:
                for way in (0, 1):
                    cols = (far_lanes if level == 0 else near_lanes)(half, steps[way])
                    landed = (r1 if level == 0 else r3)[chunk, half, part_rows(way), :]
                    span = row_span(chunk, way)
                    pbuf[span, cols] = (wide(pbuf[span, cols]) + wide(landed)).astype(jnp.bfloat16)
                    scatter_copy(chunk, level + 1, half, way).start()
            elif level == 1:
                cols, span = far_lanes(half, 0), row_span(chunk)
                total = wide(pbuf[span, cols]) + wide(r2[chunk, half, 0]) + wide(r2[chunk, half, 1])
                pbuf[span, cols] = total.astype(jnp.bfloat16)
                for way in (0, 1):
                    scatter_copy(chunk, 2, half, way).start()
            else:
                span = row_span(chunk)
                own = pl.ds(half * HALF, HALF)
                total = (
                    wide(pbuf[span, near_lanes(half, 0)])
                    + wide(r4[chunk, half, 0])
                    + wide(r4[chunk, half, 1])
                )
                out_ref[span, own] = (wide(mixed[span, own]) + total).astype(jnp.bfloat16)

    def scatter_sent(chunk, level):
        for half in (0, 1):
            for way in (0, 1):
                scatter_copy(chunk, level, half, way).wait_send()

    def dec_copy(k, arriving):
        other = lax.rem(me + k, PEERS)
        return pltpu.make_async_remote_copy(
            src_ref=dec_ref,
            dst_ref=dbuf.at[lax.rem(me - k + PEERS, PEERS) if arriving else me],
            send_sem=d_send.at[k],
            recv_sem=d_recv.at[k],
            device_id={"tok": other},
            device_id_type=MESH,
        )

    def project(chunk):
        first = chunk * tiles
        piece = jnp.concatenate(
            [abuf[(first + t) // SIDE, (first + t) % SIDE] for t in range(tiles)], axis=0
        )
        span = row_span(chunk)
        total = jnp.dot(piece, wo_ref[...], preferred_element_type=jnp.float32)
        value = (wide(resid_ref[span, :]) + total).astype(jnp.bfloat16)
        mixed[span, :] = value
        xbuf[span, near_lanes(0, 0)] = value[:, :HALF]
        xbuf[span, near_lanes(1, 0)] = value[:, HALF:]

    def normalize(chunk):
        @pl.loop(0, tiles)
        def _(t):
            span = pl.ds(pl.multiple_of(chunk * rows + t * SUB, SUB), SUB)
            total = jnp.zeros((SUB, HALF), jnp.float32)
            for block in range(D // HALF):
                value = wide(xbuf[span, block * HALF : (block + 1) * HALF])
                total = total + value * value
            scale = lax.rsqrt(jnp.sum(total, axis=-1, keepdims=True) / D + epsilon)
            owner = tenant_ref[span, :]
            to = pl.ds(pl.multiple_of(t * SUB, SUB), SUB)
            for block in range(D // HALF):
                cols = slice(block * HALF, (block + 1) * HALF)
                gain = gain_ref[3:4, cols]
                for k in (2, 1, 0):
                    gain = jnp.where(owner == k, gain_ref[k : k + 1, cols], gain)
                normed[to, cols] = (wide(xbuf[span, cols]) * scale * gain).astype(jnp.bfloat16)

    def lift(tile, width):
        cols = slice(tile * width, (tile + 1) * width)
        gate = jnp.dot(normed[...], wg_ref[:, cols], preferred_element_type=jnp.float32)
        up = jnp.dot(normed[...], wu_ref[:, cols], preferred_element_type=jnp.float32)
        hidden[:, cols] = (gate / (1.0 + jnp.exp(-gate)) * up).astype(jnp.bfloat16)

    def lower(chunk, width):
        @pl.loop(0, D // width)
        def _(tile):
            cols = pl.ds(pl.multiple_of(tile * width, width), width)
            part = jnp.dot(hidden[...], wd_ref[:, cols], preferred_element_type=jnp.float32)
            pbuf[row_span(chunk), cols] = part.astype(jnp.bfloat16)

    barrier = pltpu.get_barrier_semaphore()

    @pl.loop(1, PEERS)
    def _(k):
        pl.semaphore_signal(
            barrier, inc=1, device_id={"tok": lax.rem(me + k, PEERS)}, device_id_type=MESH
        )

    fetch_wo = pltpu.make_async_copy(wo_hbm, wo_ref, w_sem.at[0])
    fetch_wo.start()

    @pl.loop(0, att_chunks)
    def _(chunk):
        abuf[chunk * SIDE + z, x] = att_ref[pl.ds(pl.multiple_of(chunk * SUB, SUB), SUB), :]

    dbuf[me] = dec_ref[...]
    pl.semaphore_wait(barrier, PEERS - 1)

    @pl.loop(0, att_chunks)
    def _(chunk):
        gather_start(*a_args, chunk, 0)

    @pl.loop(1, PEERS)
    def _(k):
        dec_copy(k, False).start()

    @pl.loop(0, PEERS)
    def _(t):
        for half in (0, 1):
            source = pl.ds(pl.multiple_of(t * BLOCK + half * HALF, HALF), HALF)
            if half == 0:
                place = t * HALF
            else:
                place = WIDE + (t % SIDE) * (SIDE * HALF) + (t // SIDE) * HALF
            target = pl.ds(pl.multiple_of(place, HALF), HALF)
            pltpu.make_async_copy(wg_hbm.at[source, :], wg_ref.at[target, :], w_sem.at[1]).start()
            pltpu.make_async_copy(wu_hbm.at[source, :], wu_ref.at[target, :], w_sem.at[2]).start()
            pltpu.make_async_copy(wd_hbm.at[:, source], wd_ref.at[:, target], w_sem.at[3]).start()

    width = 256

    @pl.loop(0, CHUNKS + 3)
    def _(s):
        att_on = s < att_chunks
        x_on = jnp.logical_and(s >= 1, s < CHUNKS + 1)
        f_on = jnp.logical_and(s >= 2, s < CHUNKS + 2)
        p_on = s >= 3

        def progress(level):
            @pl.when(att_on)
            def _():
                gather_step(a_args, s, level)

            @pl.when(x_on)
            def _():
                gather_step(x_args, s - 1, level)

            @pl.when(p_on)
            def _():
                scatter_step(s - 3, level)

        @pl.when(s == 2)
        def _():
            pltpu.make_async_copy(wg_ref, wg_ref, w_sem.at[1]).wait()
            pltpu.make_async_copy(wu_ref, wu_ref, w_sem.at[2]).wait()
            pltpu.make_async_copy(wd_ref, wd_ref, w_sem.at[3]).wait()

        @pl.when(f_on)
        def _():
            normalize(s - 2)

        progress(0)

        @pl.when(f_on)
        def _():
            lift(0, width)

        progress(1)

        @pl.when(f_on)
        def _():
            for tile in range(1, ffw // width):
                lift(tile, width)

        progress(2)

        @pl.when(f_on)
        def _():
            lower(s - 2, 512)
            scatter_start(s - 2, 0)

        progress(3)

        @pl.when(s == 0)
        def _():
            fetch_wo.wait()

        @pl.when(s == CHUNKS - 1)
        def _():
            @pl.loop(1, PEERS)
            def _(k):
                dec_copy(k, True).wait_recv()

            for head in range(H):
                abuf[att_chunks * SIDE, 0, :, head * HD : (head + 1) * HD] = dbuf[
                    :, head, :
                ].astype(jnp.bfloat16)

        @pl.when(s < CHUNKS)
        def _():
            project(s)
            gather_start(*x_args, s, 0)

    @pl.loop(1, PEERS)
    def _(k):
        dec_copy(k, False).wait_send()

    @pl.loop(0, att_chunks)
    def _(chunk):
        for level in range(4):
            gather_sent(*a_args, chunk, level)

    @pl.loop(0, CHUNKS)
    def _(chunk):
        for level in range(4):
            gather_sent(*x_args, chunk, level)
            scatter_sent(chunk, level)


def ring_call(att, dec, resid, owner, gains, wo, w_gate, w_up, w_down):
    tokens = resid.shape[0]
    rows = tokens // CHUNKS
    ffw = w_gate.shape[1]
    vmem = pl.BlockSpec(memory_space=pltpu.VMEM)
    hbm = pl.BlockSpec(memory_space=pl.ANY)
    bf16 = jnp.bfloat16
    dma = pltpu.SemaphoreType.DMA
    return pl.pallas_call(
        ring_kernel,
        out_shape=jax.ShapeDtypeStruct((tokens, BLOCK), bf16),
        in_specs=[vmem] * 5 + [hbm] * 4,
        out_specs=vmem,
        scratch_shapes=[
            pltpu.VMEM((SIDE * SIDE + 1, SIDE, SUB, D), bf16),
            pltpu.VMEM((PEERS, H, HD), jnp.float32),
            pltpu.VMEM((tokens, D), bf16),
            pltpu.VMEM((tokens, D), bf16),
            pltpu.VMEM((tokens, BLOCK), bf16),
            pltpu.VMEM((rows, D), bf16),
            pltpu.VMEM((rows, ffw), bf16),
            pltpu.VMEM((CHUNKS, 2, rows, 4 * HALF), bf16),
            pltpu.VMEM((CHUNKS, 2, 2, rows, 4 * HALF), bf16),
            pltpu.VMEM((CHUNKS, 2, rows, HALF), bf16),
            pltpu.VMEM((CHUNKS, 2, 2, rows, HALF), bf16),
            pltpu.VMEM(wo.shape, bf16),
            pltpu.VMEM(w_gate.shape, bf16),
            pltpu.VMEM(w_up.shape, bf16),
            pltpu.VMEM(w_down.shape, bf16),
            dma((4,)),
            dma((CHUNKS, 16)),
            dma((CHUNKS, 16)),
            dma((PEERS,)),
            dma((PEERS,)),
            dma((CHUNKS, 16)),
            dma((CHUNKS, 16)),
            dma((CHUNKS, 16)),
            dma((CHUNKS, 16)),
        ],
        compiler_params=pltpu.CompilerParams(
            collective_id=1, has_side_effects=True, vmem_limit_bytes=67000000
        ),
        name="ring_layer",
    )(att, dec, resid, owner, gains, wo, w_gate, w_up, w_down)


def grouped(rows, blocks):
    count = rows.shape[0] // blocks
    rest = rows.shape[1:]
    split = rows.reshape(blocks, count, *rest)
    main = split[:, : count - 1].reshape(blocks, (count - 1) // SUB, SUB, *rest)
    main = jnp.swapaxes(main, 0, 1).reshape(blocks * (count - 1), *rest)
    return jnp.concatenate([main, split[:, count - 1]], axis=0)


def ungrouped(rows, blocks):
    count = rows.shape[0] // blocks
    rest = rows.shape[1:]
    main = rows[: blocks * (count - 1)].reshape((count - 1) // SUB, blocks, SUB, *rest)
    main = jnp.swapaxes(main, 0, 1).reshape(blocks, count - 1, *rest)
    last = rows[blocks * (count - 1) :].reshape(blocks, 1, *rest)
    return jnp.concatenate([main, last], axis=1).reshape(blocks * count, *rest)


def shards(
    pre_q,
    pre_kv,
    pre_segment,
    dec_q,
    cache,
    cache_len,
    slot_request,
    resid,
    wo,
    tenant,
    norm_gain,
    w_gate,
    w_up,
    w_down,
):
    group = H // KVH
    width = KVH * HD
    tok_index = lax.axis_index("tok")
    local_rows = pre_q.shape[0]
    segment = pre_segment[0]
    query_pos = tok_index * local_rows + jnp.arange(local_rows)
    query_seg = lax.dynamic_slice_in_dim(segment, tok_index * local_rows, local_rows)
    queries = pre_q.reshape(local_rows, KVH, group, HD)
    piece = lax.all_gather(pre_kv, "tok", axis=0, tiled=True)
    count = piece.shape[0]
    keys = piece[:, :width].reshape(count, KVH, HD)
    values = piece[:, width:].reshape(count, KVH, HD)
    key_pos = jnp.arange(count)
    allowed = (key_pos[None, :] <= query_pos[:, None]) & (segment[None, :] == query_seg[:, None])
    scores = jnp.einsum(
        "qkgd,nkd->kgqn", queries, keys, preferred_element_type=jnp.float32
    ) / math.sqrt(HD)
    scores = jnp.where(allowed, scores, -jnp.inf)
    highest = jnp.max(scores, axis=-1, keepdims=True)
    weights = jnp.exp(scores - highest).astype(jnp.bfloat16)
    totals = jnp.sum(weights.astype(jnp.float32), axis=-1)
    summed = jnp.einsum("kgqn,nkd->kgqd", weights, values, preferred_element_type=jnp.float32)
    prefill_out = (
        (summed / totals[..., None])
        .transpose(2, 0, 1, 3)
        .reshape(local_rows, D)
        .astype(jnp.bfloat16)
    )
    all_queries = lax.all_gather(dec_q, ("grp", "tok"), axis=0, tiled=True)
    slot = lax.axis_index(("grp", "tok"))
    request = slot_request[slot]
    query_row = lax.dynamic_slice_in_dim(all_queries, request, 1, 0).reshape(KVH, group, HD)
    positions = cache.shape[1]
    entries = cache[0].reshape(positions, 2, KVH, HD)
    slot_scores = jnp.einsum(
        "kgd,pkd->kgp", query_row, entries[:, 0], preferred_element_type=jnp.float32
    ) / math.sqrt(HD)
    visible = jnp.arange(positions) < cache_len[0]
    slot_scores = jnp.where(visible, slot_scores, -jnp.inf)
    slot_top = jnp.max(slot_scores, axis=-1, keepdims=True)
    slot_weights = jnp.exp(slot_scores - slot_top).astype(jnp.bfloat16)
    slot_total = jnp.sum(slot_weights.astype(jnp.float32), axis=-1)
    slot_mixed = jnp.einsum(
        "kgp,pkd->kgd", slot_weights, entries[:, 1], preferred_element_type=jnp.float32
    )
    decode_out = (slot_mixed / slot_total[..., None]).reshape(H, HD)

    blocks = lax.axis_size("tok")
    owner = grouped(tenant[0], blocks)
    owner = jnp.broadcast_to(owner[:, None], (owner.shape[0], HALF))
    pieces = norm_gain.reshape(-1, SIDE, SIDE, 2, HALF)
    first = pieces[:, :, :, 0].reshape(-1, WIDE)
    second = jnp.swapaxes(pieces[:, :, :, 1], 1, 2).reshape(-1, WIDE)
    gains = jnp.concatenate([first, second], axis=1)
    result = ring_call(
        prefill_out,
        decode_out,
        grouped(resid, blocks),
        owner,
        gains,
        wo,
        w_gate,
        w_up,
        w_down,
    )
    return ungrouped(result, blocks)


def solution(mesh):
    in_specs = (
        P(("grp", "tok"), None),
        P(("grp", "tok"), None),
        P("grp", None),
        P(("grp", "tok"), None),
        P(("grp", "tok"), None, None),
        P(("grp", "tok")),
        P(),
        P("grp", "tok"),
        P(None, "tok"),
        P("grp", None),
        P(),
        P(None, "tok"),
        P(None, "tok"),
        P("tok", None),
    )
    out_specs = P("grp", "tok")
    return jax.shard_map(shards, mesh=mesh, in_specs=in_specs, out_specs=out_specs, check_vma=False)
```

time: 469 us -> 343 us (0.73)
  waiting for transfers between devices: 363 us -> 107 us
  Pallas kernels: 0 us -> 183 us
  matrix products: 55.2 us -> 7.95 us
  starting transfers between devices: 5.6 us -> 0.04 us
    pallas_call x0 -> x1, Pallas kernels: none -> 183 us  [ring_call(): pl.pallas_call(ring_kernel, out_shape=jax.ShapeDtypeStruct((tokens, BLOCK...]
    all_gather x2 -> x0, waiting for transfers between devices: 152 us -> none  [the longest x1 76.7 us: shards(): piece = lax.all_gather(normed_part, 'tok', axis=1, tiled=True)]
    reduce_scatter x1 -> x0, waiting for transfers between devices: 94.2 us -> none  [shards(): lax.psum_scatter(lax.dot_general(w_down, hidden, (((0,), (1,)), ((), ()))...]
    dot_general x4 -> x0, matrix products: 45.9 us -> none  [the longest x1 26.3 us: shards(): lax.dot_general(w_down, hidden, (((0,), (1,)), ((), ())), preferred_eleme...]
    all_to_all x1 -> x0, waiting for transfers between devices: 7.6 us -> none  [copy_for_each(): return lax.all_to_all(copies, axis, split_axis=0, concat_axis=0, tiled=True)]
    all_to_all x1 -> x0, starting transfers between devices: 5.25 us -> none  [copy_for_each(): return lax.all_to_all(copies, axis, split_axis=0, concat_axis=0, tiled=True)]
    unnamed x13 -> x20, local copies, waits for them, and re-layouts: 11.9 us -> 9.25 us
  transfers between devices with their start and end apart: 6 -> 2, of which waited for: 6 -> 2; matrix products, arithmetic and copies ran while one was open for 2% -> 4% of each run, Pallas kernels for 0% -> 0%
where the time goes in v1:
time: 343 us; the launch traced here: 342 us
  Pallas kernels  183 us (53%)
  waiting for transfers between devices  107 us (31%)
  local copies, waits for them, and re-layouts  24.8 us (7%)
  between operations  16.4 us (5%)
  matrix products  7.95 us (2%)
  other arithmetic  3.77 us (1%)
    pallas_call x1, Pallas kernels, ring_call(): pl.pallas_call(ring_kernel, out_shape=jax.ShapeDtypeStruct((tokens, BLOCK...  183 us
    all_gather x1, waiting for transfers between devices, shards(): all_queries = lax.all_gather(dec_q, ('grp', 'tok'), axis=0, tiled=True)  57.5 us
    all_gather x1, waiting for transfers between devices, shards(): piece = lax.all_gather(pre_kv, 'tok', axis=0, tiled=True)  47.9 us
    unnamed x20, local copies, waits for them, and re-layouts  9.25 us
  transfers between devices with their start and end apart: 2, of which 2 were waited for; matrix products, arithmetic and copies ran while one was open for 4% of the time, Pallas kernels for 0%

profile of v1, /device:TPU:0, one launch (start us, length us, event | category | flops | bytes accessed | tf_op | source)
XLA Modules:
  0.0 342.5 jit_solution(3114556401274742843)
XLA Ops:
  6.5 0.0 copy-start
  6.5 0.0 all-gather.6.cloned.1.call-start
  6.5 0.7 all-gather.6.cloned.1.call-update
  7.3 0.0 all-gather.4.cloned.1.call-start
  7.3 0.7 all-gather.4.cloned.1.call-update
  8.0 1.2 dynamic_slice.10
  10.6 0.0 copy-start.5
  10.6 0.0 copy-start.4
  10.6 1.2 reshape.67
  11.8 0.0 copy-start.6
  11.9 2.2 reshape.63
  14.2 0.0 copy-done
  14.2 2.5 copy.59
  16.7 0.0 copy-start.1
  17.6 0.0 copy-done.5
  17.6 0.1 reshape_squeeze.10
  17.7 0.1 slice.55
  17.8 0.1 copy.81
  17.8 0.1 reshape.70
  17.9 0.1 reshape.71
  18.0 0.0 copy-done.4
  18.0 0.1 reshape.72
  18.1 0.1 fusion.11
  18.9 0.0 copy-done.6
  18.9 0.1 dynamic-slice_bitcast_fusion
  19.0 0.1 fusion.6
  19.1 0.8 pad_maximum_fusion.1.resid_ref
  20.0 0.6 pad_maximum_fusion.2.gain_ref
  20.6 57.5 %all-gather.6.cloned.1.call-done = bf16[128,1,4096]{2,1,0:T(2,128)(2,1)} async-done(((bf16[1,1,4096]{2,1,0:T(2,128)(2,1)}), bf16[128,1,4096]{2,1,0:T(2,128)(2,1)}) %all-gather.6.cloned.1.call-update) | async-done | bytes 1048592 | tf_op jit(solution)/shard_map/all_gather | solution.py:519
  78.1 0.8 dynamic-slice_reduce_fusion
  78.8 1.6 convert_reduce_fusion.1
  80.5 0.0 copy-done.1
  80.5 1.0 convolution_divide_fusion
  81.5 47.9 %all-gather.4.cloned.1.call-done = bf16[1024,2048]{1,0:T(8,128)(2,1)} async-done(((bf16[64,2048]{1,0:T(8,128)(2,1)}), bf16[1024,2048]{1,0:T(8,128)(2,1)}) %all-gather.4.cloned.1.call-update) | async-done | bytes 4194320 | tf_op jit(solution)/shard_map/all_gather | solution.py:499
  129.3 4.0 %fusion.10 = (bf16[1024,1024]{1,0:T(8,128)(2,1)S(1)}, bf16[1024,1024]{1,0:T(8,128)(2,1)}) fusion(bf16[1024,2048]{1,0:T(8,128)(2,1)} %all-gather.4.cloned.1.call-done), kind=kLoop, calls=%fused_computation.32 | loop fusion | bytes 8388608 | tf_op jit(solution)/shard_map/slice | solution.py:501
  133.3 0.0 copy-start.3
  133.3 4.0 %copy.77 = bf16[1024,1024]{0,1:T(8,128)(2,1)} copy(bf16[1024,1024]{1,0:T(8,128)(2,1)} %get-tuple-element.6) | data formatting | bytes 4194304
  137.3 2.6 copy.76
  139.9 0.0 copy-done.3
  139.9 3.2 fusion
  143.1 0.0 copy-start.2
  143.1 2.1 convert_reduce_fusion
  145.2 0.0 copy-done.2
  145.2 2.1 fusion.2
  147.4 0.4 copy.58
  147.8 1.2 convert_element_type.20.att_ref
  149.0 1.0 broadcast_in_dim.33.tenant_ref
  150.0 182.8 %ring_layer.1 = bf16[1040,256]{1,0:T(8,128)(2,1)} custom-call(bf16[64,4096]{1,0:T(8,128)(2,1)} %convert_element_type.20.att_ref, f32[32,128]{1,0:T(8,128)} %bitcast.89, bf16[1040,256]{1,0:T(8,128)(2,1)} %pad_maximum_fusion.1.resid_ref, s32[1040,128]{1,0:T(8,128)} %broadcast_in_dim.33.tenant_ref, f32[4,4096]{1,0:T(4,128)} %pad_maximum_fusion.2.gain_ref, ...), custom_call_target="tpu_custom_call" | custom-call | tf_op jit(solution)/shard_map/ring_layer/pallas_call | solution.py:419
  332.8 0.7 slice_bitcast_fusion.4
  333.5 1.1 slice.46
  334.7 1.0 reshape.77
  (15 shorter events, 0.3 us)
Async XLA Ops:
  6.5 7.6 %copy-start = (bf16[1,512,2048]{2,1,0:T(8,128)(2,1)S(1)}, bf16[1,512,2048]{2,1,0:T(8,128)(2,1)}, u32[]{:S(2)}) copy-start(bf16[1,512,2048]{2,1,0:T(8,128)(2,1)} %param.18) | copy-start | bytes 6291460
  6.5 71.5 %all-gather.6.cloned.1.call-start = ((), (), s32[]{:S(2)}) async-start(), calls=%async_computation.1 | async-start | bytes 2113536 | tf_op jit(solution)/shard_map/all_gather | solution.py:519
  7.3 122.1 %all-gather.4.cloned.1.call-start = ((), (), s32[]{:S(2)}) async-start(), calls=%async_computation | async-start | bytes 4456448 | tf_op jit(solution)/shard_map/all_gather | solution.py:499
  10.6 7.0 %copy-start.5 = (s32[1,1040]{1,0:T(1,128)S(1)}, s32[1,1040]{1,0:T(1,128)}, u32[]{:S(2)}) copy-start(s32[1,1040]{1,0:T(1,128)} %param.23) | copy-start | bytes 12484
  10.6 7.4 %copy-start.4 = (f32[4,4096]{1,0:T(4,128)S(1)}, f32[4,4096]{1,0:T(4,128)}, u32[]{:S(2)}) copy-start(f32[4,4096]{1,0:T(4,128)} %param.24) | copy-start | bytes 196612
  11.8 7.1 %copy-start.6 = (s32[1,1024]{1,0:T(1,128)S(1)}, s32[1,1024]{1,0:T(1,128)}, u32[]{:S(2)}) copy-start(s32[1,1024]{1,0:T(1,128)} %param.16) | copy-start | bytes 12292
  16.7 63.8 %copy-start.1 = (bf16[1,512,2048]{1,2,0:T(8,128)(2,1)S(1)}, bf16[1,512,2048]{1,2,0:T(8,128)(2,1)}, u32[]{:S(2)}) copy-start(bf16[1,512,2048]{1,2,0:T(8,128)(2,1)} %copy.59) | copy-start | bytes 6291460
  133.3 6.6 %copy-start.3 = (bf16[64,8,4,128]{3,2,1,0:T(4,128)(2,1)S(1)}, bf16[64,8,4,128]{3,2,1,0:T(4,128)(2,1)}, u32[]{:S(2)}) copy-start(bf16[64,8,4,128]{3,2,1,0:T(4,128)(2,1)} %reshape.63) | copy-start | bytes 1572868
  143.1 2.1 copy-start.2
Sparse Core Ops, SparseCore 0:
  10.3 67.6 all-gather.5
  80.2 49.1 all-gather.3

commit v2 on v1

--- a/solution.py
+++ b/solution.py
@@ -454,6 +454,303 @@
     )(att, dec, resid, owner, gains, wo, w_gate, w_up, w_down)
 
 
+def attend_kernel(
+    length_ref,
+    request_ref,
+    query_ref,
+    pair_ref,
+    segment_ref,
+    dec_ref,
+    cache_hbm,
+    att_ref,
+    own_ref,
+    kbuf,
+    cbuf,
+    column,
+    outgoing,
+    incoming,
+    bias,
+    c_sem,
+    k_send,
+    k_recv,
+    g_send,
+    g_recv,
+    q_send,
+    q_recv,
+):
+    me = lax.axis_index("tok")
+    grp = lax.axis_index("grp")
+    groups = column.shape[0]
+    z, x = me // SIDE, me % SIDE
+    rows = query_ref.shape[0]
+    width = KVH * HD
+    group = H // KVH
+    pieces = k_send.shape[0]
+    heads = KVH // pieces
+    steps = (1, -1)
+
+    def hop(value, step):
+        return lax.rem(value + step + SIDE, SIDE)
+
+    def neighbour(axis, step):
+        if axis == 0:
+            return z * SIDE + hop(x, step)
+        return hop(z, step) * SIDE + x
+
+    def block(piece, half, offset, level, part):
+        cols = pl.ds(half * width + piece * heads * HD, heads * HD)
+        span = pl.ds(0, rows) if part is None else pl.ds(part * (rows // 2), rows // 2)
+        if level < 2:
+            if half == 0:
+                return kbuf.at[z, hop(x, offset), span, cols]
+            return kbuf.at[hop(z, offset), x, span, cols]
+        if half == 0:
+            return kbuf.at[hop(z, offset), :, span, cols]
+        return kbuf.at[:, hop(x, offset), span, cols]
+
+    def copy(piece, level, half, way, arriving):
+        step = steps[way]
+        axis = half if level < 2 else 1 - half
+        if level % 2 == 0:
+            ref = block(piece, half, -step if arriving else 0, level, None)
+        else:
+            ref = block(piece, half, -2 * step if arriving else -step, level, way)
+        index = level * 4 + half * 2 + way
+        return pltpu.make_async_remote_copy(
+            src_ref=ref,
+            dst_ref=ref,
+            send_sem=k_send.at[piece, index],
+            recv_sem=k_recv.at[piece, index],
+            device_id={"tok": neighbour(axis, step)},
+            device_id_type=MESH,
+        )
+
+    def start(piece, level):
+        for half in (0, 1):
+            for way in (0, 1):
+                copy(piece, level, half, way, False).start()
+
+    def step(piece, level):
+        for half in (0, 1):
+            for way in (0, 1):
+                copy(piece, level, half, way, True).wait_recv()
+        if level < 3:
+            start(piece, level + 1)
+
+    def group_copy(k, arriving):
+        source = lax.rem(grp - k + groups, groups) if arriving else grp
+        return pltpu.make_async_remote_copy(
+            src_ref=dec_ref,
+            dst_ref=column.at[source],
+            send_sem=g_send.at[k],
+            recv_sem=g_recv.at[k],
+            device_id={"grp": lax.rem(grp + k, groups)},
+            device_id_type=MESH,
+        )
+
+    def query_copy(k, arriving):
+        other = lax.rem(me + k, PEERS)
+        source = lax.rem(me - k + PEERS, PEERS) if arriving else me
+        return pltpu.make_async_remote_copy(
+            src_ref=outgoing.at[other],
+            dst_ref=incoming.at[source],
+            send_sem=q_send.at[k],
+            recv_sem=q_recv.at[k],
+            device_id={"tok": other},
+            device_id_type=MESH,
+        )
+
+    barrier = pltpu.get_barrier_semaphore()
+    fetch = pltpu.make_async_copy(cache_hbm, cbuf, c_sem)
+    fetch.start()
+
+    @pl.loop(1, PEERS)
+    def _(k):
+        pl.semaphore_signal(
+            barrier, inc=1, device_id={"tok": lax.rem(me + k, PEERS)}, device_id_type=MESH
+        )
+
+    @pl.loop(1, groups)
+    def _(k):
+        pl.semaphore_signal(
+            barrier, inc=1, device_id={"grp": lax.rem(grp + k, groups)}, device_id_type=MESH
+        )
+
+    kbuf[z, x] = pair_ref[...]
+    column[grp] = dec_ref[...]
+    pl.semaphore_wait(barrier, PEERS + groups - 2)
+
+    @pl.loop(1, groups)
+    def _(k):
+        group_copy(k, False).start()
+
+    for piece in range(pieces):
+        start(piece, 0)
+
+    window = 10
+    first = 2 * (jnp.maximum(me - 8, 0) // 2)
+    span = window * rows
+    near = pl.ds(pl.multiple_of((me // 2) * (2 * rows), 2 * rows), 2 * rows)
+    mine = segment_ref[:, near].astype(jnp.float32)
+    turned = jnp.transpose(jnp.broadcast_to(mine, (2 * rows, 2 * rows)))
+    query_seg = jnp.where(me % 2 == 1, turned[rows:], turned[:rows])[:, :1]
+    seen = pl.ds(pl.multiple_of(first * rows, 2 * rows), span)
+    key_seg = segment_ref[:, seen].astype(jnp.float32)
+    query_pos = me * rows + lax.broadcasted_iota(jnp.int32, (rows, span), 0)
+    key_pos = first * rows + lax.broadcasted_iota(jnp.int32, (rows, span), 1)
+    allowed = (key_pos <= query_pos) & (query_seg == key_seg)
+    bias[...] = jnp.where(allowed, 0.0, -jnp.inf)
+
+    @pl.loop(1, groups)
+    def _(k):
+        group_copy(k, True).wait_recv()
+
+    @pl.loop(0, PEERS)
+    def _(t):
+        request = request_ref[grp * PEERS + t]
+        row = column[request // PEERS]
+        held = request % PEERS == me
+        outgoing[t] = jnp.where(held, row.astype(jnp.float32), 0.0).astype(jnp.bfloat16)
+
+    @pl.loop(1, PEERS)
+    def _(k):
+        query_copy(k, False).start()
+
+    incoming[me] = outgoing[me]
+    scale = 1.0 / math.sqrt(HD)
+
+    def prefill(piece):
+        @pl.loop(0, heads)
+        def _(i):
+            head = piece * heads + i
+
+            def joined(base):
+                cols = pl.ds(pl.multiple_of(base + head * HD, HD), HD)
+                return jnp.concatenate(
+                    [
+                        kbuf[(first + b) // SIDE, (first + b) % SIDE, :, cols]
+                        for b in range(window)
+                    ],
+                    axis=0,
+                )
+
+            keys, values = joined(0), joined(width)
+            for j in range(group):
+                cols = pl.ds(pl.multiple_of((head * group + j) * HD, HD), HD)
+                scores = lax.dot_general(
+                    query_ref[:, cols],
+                    keys,
+                    (((1,), (1,)), ((), ())),
+                    preferred_element_type=jnp.float32,
+                )
+                scores = scores * scale + bias[...]
+                top = jnp.max(scores, axis=-1, keepdims=True)
+                weights = jnp.exp(scores - top).astype(jnp.bfloat16)
+                total = jnp.sum(weights.astype(jnp.float32), axis=-1, keepdims=True)
+                summed = jnp.dot(weights, values, preferred_element_type=jnp.float32)
+                att_ref[:, cols] = (summed / total).astype(jnp.bfloat16)
+
+    def decode():
+        query = incoming[0].astype(jnp.float32)
+        for t in range(1, PEERS):
+            query = query + incoming[t].astype(jnp.float32)
+        query = query.astype(jnp.bfloat16)
+        count = cbuf.shape[0]
+        owner = lax.broadcasted_iota(jnp.int32, (H, count), 0) // group
+        scores = jnp.zeros((H, count), jnp.float32)
+        for head in range(KVH):
+            part = lax.dot_general(
+                query,
+                cbuf[:, head * HD : (head + 1) * HD],
+                (((1,), (1,)), ((), ())),
+                preferred_element_type=jnp.float32,
+            )
+            scores = jnp.where(owner == head, part, scores)
+        visible = lax.broadcasted_iota(jnp.int32, (H, count), 1) < length_ref[0]
+        scores = jnp.where(visible, scores * scale, -jnp.inf)
+        top = jnp.max(scores, axis=-1, keepdims=True)
+        weights = jnp.exp(scores - top).astype(jnp.bfloat16)
+        total = jnp.sum(weights.astype(jnp.float32), axis=-1, keepdims=True)
+        owner = lax.broadcasted_iota(jnp.int32, (H, HD), 0) // group
+        summed = jnp.zeros((H, HD), jnp.float32)
+        for head in range(KVH):
+            base = width + head * HD
+            part = jnp.dot(
+                weights, cbuf[:, base : base + HD], preferred_element_type=jnp.float32
+            )
+            summed = jnp.where(owner == head, part, summed)
+        own_ref[...] = summed / total
+
+    for wave in range(pieces + 3):
+        for level in range(4):
+            piece = wave - level
+            if 0 <= piece < pieces:
+                step(piece, level)
+        if wave == 2:
+            fetch.wait()
+
+            @pl.loop(1, PEERS)
+            def _(k):
+                query_copy(k, True).wait_recv()
+
+            decode()
+        if wave >= 3:
+            prefill(wave - 3)
+
+    @pl.loop(1, groups)
+    def _(k):
+        group_copy(k, False).wait_send()
+
+    @pl.loop(1, PEERS)
+    def _(k):
+        query_copy(k, False).wait_send()
+
+    @pl.loop(0, pieces)
+    def _(piece):
+        for level in range(4):
+            for half in (0, 1):
+                for way in (0, 1):
+                    copy(piece, level, half, way, False).wait_send()
+
+
+def attend_call(length, request, queries, pairs, segment, dec, cache):
+    rows = queries.shape[0]
+    groups = lax.axis_size("grp")
+    pieces = 4
+    vmem = pl.BlockSpec(memory_space=pltpu.VMEM)
+    smem = pl.BlockSpec(memory_space=pltpu.SMEM)
+    bf16 = jnp.bfloat16
+    dma = pltpu.SemaphoreType.DMA
+    return pl.pallas_call(
+        attend_kernel,
+        out_shape=(
+            jax.ShapeDtypeStruct((rows, D), bf16),
+            jax.ShapeDtypeStruct((H, HD), jnp.float32),
+        ),
+        in_specs=[smem, smem, vmem, vmem, vmem, vmem, pl.BlockSpec(memory_space=pl.ANY)],
+        out_specs=(vmem, vmem),
+        scratch_shapes=[
+            pltpu.VMEM((SIDE, SIDE, rows, pairs.shape[1]), bf16),
+            pltpu.VMEM(cache.shape, bf16),
+            pltpu.VMEM((groups, H, HD), bf16),
+            pltpu.VMEM((PEERS, H, HD), bf16),
+            pltpu.VMEM((PEERS, H, HD), bf16),
+            pltpu.VMEM((rows, 10 * rows), jnp.float32),
+            dma,
+            dma((pieces, 16)),
+            dma((pieces, 16)),
+            dma((groups,)),
+            dma((groups,)),
+            dma((PEERS,)),
+            dma((PEERS,)),
+        ],
+        compiler_params=pltpu.CompilerParams(
+            collective_id=2, has_side_effects=True, vmem_limit_bytes=40000000
+        ),
+        name="attend",
+    )(length, request, queries, pairs, segment, dec, cache)
+
+
 def grouped(rows, blocks):
     count = rows.shape[0] // blocks
     rest = rows.shape[1:]
@@ -488,53 +785,15 @@
     w_up,
     w_down,
 ):
-    group = H // KVH
-    width = KVH * HD
-    tok_index = lax.axis_index("tok")
-    local_rows = pre_q.shape[0]
-    segment = pre_segment[0]
-    query_pos = tok_index * local_rows + jnp.arange(local_rows)
-    query_seg = lax.dynamic_slice_in_dim(segment, tok_index * local_rows, local_rows)
-    queries = pre_q.reshape(local_rows, KVH, group, HD)
-    piece = lax.all_gather(pre_kv, "tok", axis=0, tiled=True)
-    count = piece.shape[0]
-    keys = piece[:, :width].reshape(count, KVH, HD)
-    values = piece[:, width:].reshape(count, KVH, HD)
-    key_pos = jnp.arange(count)
-    allowed = (key_pos[None, :] <= query_pos[:, None]) & (segment[None, :] == query_seg[:, None])
-    scores = jnp.einsum(
-        "qkgd,nkd->kgqn", queries, keys, preferred_element_type=jnp.float32
-    ) / math.sqrt(HD)
-    scores = jnp.where(allowed, scores, -jnp.inf)
-    highest = jnp.max(scores, axis=-1, keepdims=True)
-    weights = jnp.exp(scores - highest).astype(jnp.bfloat16)
-    totals = jnp.sum(weights.astype(jnp.float32), axis=-1)
-    summed = jnp.einsum("kgqn,nkd->kgqd", weights, values, preferred_element_type=jnp.float32)
-    prefill_out = (
-        (summed / totals[..., None])
-        .transpose(2, 0, 1, 3)
-        .reshape(local_rows, D)
-        .astype(jnp.bfloat16)
+    prefill_out, decode_out = attend_call(
+        cache_len,
+        slot_request,
+        pre_q,
+        pre_kv,
+        pre_segment,
+        dec_q.reshape(H, HD),
+        cache[0],
     )
-    all_queries = lax.all_gather(dec_q, ("grp", "tok"), axis=0, tiled=True)
-    slot = lax.axis_index(("grp", "tok"))
-    request = slot_request[slot]
-    query_row = lax.dynamic_slice_in_dim(all_queries, request, 1, 0).reshape(KVH, group, HD)
-    positions = cache.shape[1]
-    entries = cache[0].reshape(positions, 2, KVH, HD)
-    slot_scores = jnp.einsum(
-        "kgd,pkd->kgp", query_row, entries[:, 0], preferred_element_type=jnp.float32
-    ) / math.sqrt(HD)
-    visible = jnp.arange(positions) < cache_len[0]
-    slot_scores = jnp.where(visible, slot_scores, -jnp.inf)
-    slot_top = jnp.max(slot_scores, axis=-1, keepdims=True)
-    slot_weights = jnp.exp(slot_scores - slot_top).astype(jnp.bfloat16)
-    slot_total = jnp.sum(slot_weights.astype(jnp.float32), axis=-1)
-    slot_mixed = jnp.einsum(
-        "kgp,pkd->kgd", slot_weights, entries[:, 1], preferred_element_type=jnp.float32
-    )
-    decode_out = (slot_mixed / slot_total[..., None]).reshape(H, HD)
-
     blocks = lax.axis_size("tok")
     owner = grouped(tenant[0], blocks)
     owner = jnp.broadcast_to(owner[:, None], (owner.shape[0], HALF))

time: 343 us -> 232 us (0.68)
  waiting for transfers between devices: 107 us -> 0 us
  Pallas kernels: 183 us -> 223 us
  local copies, waits for them, and re-layouts: 24.8 us -> 6.57 us
  between operations: 16.4 us -> 0.9 us
  matrix products: 7.95 us -> 0 us
    all_gather x2 -> x0, waiting for transfers between devices: 105 us -> none  [the longest x1 57.5 us: shards(): all_queries = lax.all_gather(dec_q, ('grp', 'tok'), axis=0, tiled=True)]
    pallas_call x0 -> x1, Pallas kernels: none -> 43.8 us  [attend_call(): pl.pallas_call(attend_kernel, out_shape=(jax.ShapeDtypeStruct((rows, D),...]
    unnamed x20 -> x25, local copies, waits for them, and re-layouts: 9.25 us -> 1.71 us
    dot_general x3 -> x0, matrix products: 6.32 us -> none  [the longest x1 3.18 us: shards(): jnp.einsum('qkgd,nkd->kgqn', queries, keys, preferred_element_type=jnp.fl...]
    slice x1 -> x0, local copies, waits for them, and re-layouts: 3.99 us -> none  [shards(): keys = piece[:, :width].reshape(count, KVH, HD)]
    pallas_call x1, Pallas kernels: 183 us -> 179 us  [ring_call(): pl.pallas_call(ring_kernel, out_shape=jax.ShapeDtypeStruct((tokens, BLOCK...]
  transfers between devices with their start and end apart: 2 -> 0, of which waited for: 2 -> 0; matrix products, arithmetic and copies ran while one was open for 4% -> 0% of each run, Pallas kernels for 0% -> 0%
where the time goes in v2:
time: 232 us
  Pallas kernels  223 us (96%)
  local copies, waits for them, and re-layouts  6.57 us (3%)
    pallas_call x1, Pallas kernels, ring_call(): pl.pallas_call(ring_kernel, out_shape=jax.ShapeDtypeStruct((tokens, BLOCK...  179 us
    pallas_call x1, Pallas kernels, attend_call(): pl.pallas_call(attend_kernel, out_shape=(jax.ShapeDtypeStruct((rows, D),...  43.8 us

profile of v2, /device:TPU:0, one launch (start us, length us, event | category | flops | bytes accessed | tf_op | source)
XLA Modules:
  0.0 231.8 jit_solution(15653814314630655347)
XLA Ops:
  0.0 1.2 reshape.38
  1.3 0.0 copy-start.10
  1.3 0.0 copy-start.1
  1.3 0.0 copy-start.8
  1.4 0.0 copy-start.9
  1.4 0.0 copy-start
  1.4 0.0 copy-start.3
  1.4 0.0 copy-start.5
  1.4 0.0 copy-start.6
  1.4 0.8 pad_maximum_fusion.1.resid_ref
  2.3 0.0 copy-done.10
  2.3 0.1 reshape_squeeze.6
  2.4 0.1 reshape.41
  2.5 0.1 reshape.42
  2.6 0.1 slice.35
  2.6 0.1 copy.36
  2.7 1.0 broadcast_in_dim.2.tenant_ref
  3.7 0.0 copy-done.8
  3.7 0.1 reshape.43
  3.8 0.1 fusion
  3.9 0.6 pad_maximum_fusion.2.gain_ref
  4.6 0.0 copy-done.9
  4.6 0.1 reduce
  5.3 0.0 copy-done.1
  5.3 0.0 copy-done
  5.3 0.0 copy-done.3
  5.3 0.0 copy-done.5
  5.3 0.0 copy-done.6
  5.3 43.8 %attend.1 = (bf16[64,4096]{1,0:T(8,128)(2,1)S(1)}, f32[32,128]{1,0:T(8,128)S(1)}) custom-call(s32[1]{0:T(128)S(6)} %copy.43.length_ref, s32[128]{0:T(128)S(1)} %copy-done.6, bf16[64,4096]{1,0:T(8,128)(2,1)S(1)} %copy-done.1, bf16[64,2048]{1,0:T(8,128)(2,1)S(1)} %copy-done.3, s32[1,1024]{1,0:T(1,128)S(1)} %copy-done.5, bf16[32,128]{1,0:T(8,128)(2,1)S(1)} %bitcast.27, ...), custom_call_target="tpu_custom_call" | custom-call | tf_op jit(solution)/shard_map/attend/pallas_call | solution.py:724
  49.2 0.0 copy-start.2
  49.2 0.8 copy-done.2
  50.0 0.0 copy-start.4
  50.0 0.6 copy-done.4
  50.6 178.9 %ring_layer.1 = bf16[1040,256]{1,0:T(8,128)(2,1)} custom-call(bf16[64,4096]{1,0:T(8,128)(2,1)} %copy-done.2, f32[32,128]{1,0:T(8,128)} %copy-done.4, bf16[1040,256]{1,0:T(8,128)(2,1)} %pad_maximum_fusion.1.resid_ref, s32[1040,128]{1,0:T(8,128)} %broadcast_in_dim.2.tenant_ref, f32[4,4096]{1,0:T(4,128)} %pad_maximum_fusion.2.gain_ref, ...), custom_call_target="tpu_custom_call" | custom-call | tf_op jit(solution)/shard_map/ring_layer/pallas_call | solution.py:419
  229.5 0.0 slice-start
  229.5 0.0 copy-start.7
  229.5 1.0 slice-done
  230.6 0.2 copy-done.7
  230.8 1.0 reshape.48
  (14 shorter events, 0.3 us)
Async XLA Ops:
  1.3 1.0 copy-start.10
  1.3 4.0 %copy-start.1 = (bf16[64,4096]{1,0:T(8,128)(2,1)S(1)}, bf16[64,4096]{1,0:T(8,128)(2,1)}, u32[]{:S(2)}) copy-start(bf16[64,4096]{1,0:T(8,128)(2,1)} %query_ref.1) | copy-start | bytes 1572868
  1.3 2.4 %copy-start.8 = (f32[4,4096]{1,0:T(4,128)S(1)}, f32[4,4096]{1,0:T(4,128)}, u32[]{:S(2)}) copy-start(f32[4,4096]{1,0:T(4,128)} %param.24) | copy-start | bytes 196612
  1.4 3.2 %copy-start.9 = (bf16[1,4096]{1,0:T(2,128)(2,1)S(1)}, bf16[1,4096]{1,0:T(2,128)(2,1)}, u32[]{:S(2)}) copy-start(bf16[1,4096]{1,0:T(2,128)(2,1)} %param.17) | copy-start | bytes 24580
  1.4 3.9 %copy-start = (bf16[1,512,2048]{2,1,0:T(8,128)(2,1)S(1)}, bf16[1,512,2048]{2,1,0:T(8,128)(2,1)}, u32[]{:S(2)}) copy-start(bf16[1,512,2048]{2,1,0:T(8,128)(2,1)} %param.18) | copy-start | bytes 6291460
  1.4 3.9 %copy-start.3 = (bf16[64,2048]{1,0:T(8,128)(2,1)S(1)}, bf16[64,2048]{1,0:T(8,128)(2,1)}, u32[]{:S(2)}) copy-start(bf16[64,2048]{1,0:T(8,128)(2,1)} %pair_ref.1) | copy-start | bytes 786436
  1.4 3.9 %copy-start.5 = (s32[1,1024]{1,0:T(1,128)S(1)}, s32[1,1024]{1,0:T(1,128)}, u32[]{:S(2)}) copy-start(s32[1,1024]{1,0:T(1,128)} %segment_ref.1) | copy-start | bytes 12292
  1.4 3.9 %copy-start.6 = (s32[128]{0:T(128)S(1)}, s32[128]{0:T(128)}, u32[]{:S(2)}) copy-start(s32[128]{0:T(128)} %request_ref.1) | copy-start | bytes 1540
  49.2 0.8 copy-start.2
  50.0 0.6 copy-start.4
  229.5 1.0 slice-start
  229.5 1.2 copy-start.7

commit v3 on v0

v3 whole, which is shorter than its diff:
```python
import functools
import math

import jax
import jax.numpy as jnp
from jax import lax
from jax.experimental import pallas as pl
from jax.experimental.pallas import tpu as pltpu
from jax.sharding import PartitionSpec as P

D = 4096
H = 32
KVH = 8
HD = 128
SIDE = 4
PEERS = SIDE * SIDE
BLOCK = D // PEERS
HALF = BLOCK // 2
WIDE = D // 2
QUAD = SIDE * HALF
SUB = 16
PIECES = 4
WINDOW = 10
CORES = 2

epsilon = 1e-05
MESH = pl.DeviceIdType.MESH
WAYS = (1, -1)


def layer_kernel(
    length_ref,
    request_ref,
    query_ref,
    pair_ref,
    segment_ref,
    dec_ref,
    cache_hbm,
    resid_ref,
    tenant_ref,
    gain_ref,
    wo_hbm,
    wg_hbm,
    wu_hbm,
    wd_hbm,
    out_ref,
    abuf,
    wbuf,
    xbuf,
    pbuf,
    normed,
    hidden,
    r1,
    r2,
    r3,
    r4,
    wg_ref,
    wu_ref,
    wd_ref,
    bias,
    column,
    outgoing,
    incoming,
    own,
    dbuf,
    rbuf,
    xdec,
    pdec,
    rdec,
    w_sem,
    k_send,
    k_recv,
    g_send,
    g_recv,
    q_send,
    q_recv,
    d_send,
    d_recv,
    a_send,
    a_recv,
    wz_send,
    wz_recv,
    wy_send,
    wy_recv,
    wc_send,
    wc_recv,
    b_send,
    b_recv,
    e_send,
    e_recv,
    x_send,
    x_recv,
    p_send,
    p_recv,
    f_send,
    f_recv,
):
    me = lax.axis_index("tok")
    grp = lax.axis_index("grp")
    groups = column.shape[0]
    z, x = me // SIDE, me % SIDE
    y, core = grp // CORES, grp % CORES
    rows = query_ref.shape[0]
    tall = SIDE * rows
    width = KVH * HD
    group = H // KVH
    heads = KVH // PIECES
    ffw = wg_ref.shape[1]
    slab = D // groups
    scale = 1.0 / math.sqrt(HD)

    def hop(value, step):
        return lax.rem(value + step + SIDE, SIDE)

    def neighbour(axis, step):
        if axis == 0:
            return {"tok": z * SIDE + hop(x, step)}
        if axis == 1:
            return {"tok": hop(z, step) * SIDE + x}
        return {"grp": hop(y, step) * CORES + core}

    def remote(src, dst, sent, landed, peer):
        return pltpu.make_async_remote_copy(
            src_ref=src,
            dst_ref=dst,
            send_sem=sent,
            recv_sem=landed,
            device_id=peer,
            device_id_type=MESH,
        )

    def lanes(base, size):
        return pl.ds(pl.multiple_of(base, HALF), size)

    def wide(value):
        return value.astype(jnp.float32)

    def inner(part):
        if part is None:
            return pl.ds(0, rows)
        return pl.ds(part * (rows // 2), rows // 2)

    def k_block(piece, half, offset, level, part):
        cols = pl.ds(half * width + piece * heads * HD, heads * HD)
        span = inner(part)
        if level < 2:
            if half == 0:
                return pbuf.at[z, hop(x, offset), span, cols]
            return pbuf.at[hop(z, offset), x, span, cols]
        if half == 0:
            return pbuf.at[hop(z, offset), :, span, cols]
        return pbuf.at[:, hop(x, offset), span, cols]

    def x_block(chunk, half, offset, level, part):
        span = inner(part)
        if level < 2:
            if half == 0:
                return xbuf.at[chunk, z, span, lanes(hop(x, offset) * QUAD, QUAD)]
            return xbuf.at[chunk, hop(z, offset), span, lanes(WIDE + x * QUAD, QUAD)]
        if half == 0:
            return xbuf.at[chunk, hop(z, offset), span, pl.ds(0, WIDE)]
        return xbuf.at[chunk, :, span, lanes(WIDE + hop(x, offset) * QUAD, QUAD)]

    def gather_copy(block, sends, recvs, chunk, level, half, way, arriving):
        step = WAYS[way]
        axis = half if level < 2 else 1 - half
        if level % 2 == 0:
            ref = block(chunk, half, -step if arriving else 0, level, None)
        else:
            ref = block(chunk, half, -2 * step if arriving else -step, level, way)
        index = level * 4 + half * 2 + way
        return remote(
            ref, ref, sends.at[chunk, index], recvs.at[chunk, index], neighbour(axis, step)
        )

    def each(make):
        for half in (0, 1):
            for way in (0, 1):
                make(half, way)

    def gather_start(args, chunk, level):
        each(lambda half, way: gather_copy(*args, chunk, level, half, way, False).start())

    def gather_step(args, chunk, level):
        each(lambda half, way: gather_copy(*args, chunk, level, half, way, True).wait_recv())
        if level < 3:
            gather_start(args, chunk, level + 1)

    def gather_sent(args, chunk, level):
        each(lambda half, way: gather_copy(*args, chunk, level, half, way, False).wait_send())

    k_args = (k_block, k_send, k_recv)
    x_args = (x_block, x_send, x_recv)

    def a_copy(piece, level, way, arriving):
        step = WAYS[way]
        offset = -step * (level + 1) if arriving else -step * level
        base = hop(x, offset) * rows
        count = rows
        if level == 1:
            base = base + way * (rows // 2)
            count = rows // 2
        cols = pl.ds(piece * (D // PIECES), D // PIECES)
        ref = abuf.at[pl.ds(pl.multiple_of(base, SUB), count), cols]
        index = level * 2 + way
        return remote(
            ref, ref, a_send.at[piece, index], a_recv.at[piece, index], neighbour(0, step)
        )

    def slab_rows(offset, part=None):
        base = (hop(y, offset) * CORES + core) * slab
        if part is None:
            return pl.ds(pl.multiple_of(base, slab // 2), slab)
        return pl.ds(pl.multiple_of(base + part * (slab // 2), slab // 2), slab // 2)

    def wz_copy(level, way, arriving):
        step = WAYS[way]
        offset = -step * (level + 1) if arriving else -step * level
        span = slab_rows(0, way if level == 1 else None)
        dst = wbuf.at[hop(z, offset), span, :]
        src = wo_hbm.at[span, :] if level == 0 and not arriving else dst
        index = level * 2 + way
        return remote(src, dst, wz_send.at[index], wz_recv.at[index], neighbour(1, step))

    def wy_copy(other, level, way, arriving):
        step = WAYS[way]
        offset = -step * (level + 1) if arriving else -step * level
        span = slab_rows(offset, way if level == 1 else None)
        ref = wbuf.at[hop(z, other), span, :]
        index = (other - 1) * 4 + level * 2 + way
        return remote(ref, ref, wy_send.at[index], wy_recv.at[index], neighbour(2, step))

    def wc_copy(other, offset, arriving):
        base = hop(y, offset) * CORES + (1 - core if arriving else core)
        ref = wbuf.at[hop(z, other), pl.ds(pl.multiple_of(base * slab, slab), slab), :]
        index = (other - 1) * 4 + offset + 1
        peer = {"grp": y * CORES + 1 - core}
        return remote(ref, ref, wc_send.at[index], wc_recv.at[index], peer)

    def group_copy(k, arriving):
        source = lax.rem(grp - k + groups, groups) if arriving else grp
        peer = {"grp": lax.rem(grp + k, groups)}
        return remote(dec_ref, column.at[source], g_send.at[k], g_recv.at[k], peer)

    def ahead(k):
        return lax.rem(me + k, PEERS)

    def behind(k):
        return lax.rem(me - k + PEERS, PEERS)

    def query_copy(k, arriving):
        dst = incoming.at[behind(k) if arriving else me]
        return remote(outgoing.at[ahead(k)], dst, q_send.at[k], q_recv.at[k], {"tok": ahead(k)})

    def dec_copy(k, arriving):
        dst = dbuf.at[behind(k) if arriving else me]
        return remote(own, dst, d_send.at[k], d_recv.at[k], {"tok": ahead(k)})

    def fdec_copy(k, arriving):
        dst = rdec.at[behind(k) if arriving else me]
        return remote(pdec.at[ahead(k)], dst, f_send.at[k], f_recv.at[k], {"tok": ahead(k)})

    def base_copies(k, arriving):
        to = hop(z, k)
        slot = hop(z, -k) if arriving else z
        start = pl.ds(pl.multiple_of(to * tall, tall), tall)
        peer = {"tok": to * SIDE + x}
        last = pl.ds(PEERS * rows, PEERS)
        return (
            remote(
                resid_ref.at[start, :],
                rbuf.at[slot, pl.ds(0, tall), :],
                b_send.at[2 * k],
                b_recv.at[2 * k],
                peer,
            ),
            remote(
                resid_ref.at[last, :],
                rbuf.at[slot, pl.ds(tall, PEERS), :],
                b_send.at[2 * k + 1],
                b_recv.at[2 * k + 1],
                peer,
            ),
        )

    def xdec_copies(k, arriving):
        owner = hop(x, -k) if arriving else x
        peer = {"tok": z * SIDE + hop(x, k)}
        copies = []
        for half in (0, 1):
            ref = xdec.at[:, lanes(half * WIDE + owner * QUAD, QUAD)]
            index = 2 * k + half
            copies.append(remote(ref, ref, e_send.at[index], e_recv.at[index], peer))
        return copies

    def near_lanes(half, offset):
        if half == 0:
            return lanes(z * QUAD + hop(x, offset) * HALF, HALF)
        return lanes(WIDE + x * QUAD + hop(z, offset) * HALF, HALF)

    def far_lanes(half, offset):
        if half == 0:
            return lanes(hop(z, offset) * QUAD, QUAD)
        return lanes(WIDE + hop(x, offset) * QUAD, QUAD)

    def scatter_copy(chunk, level, half, way):
        step = WAYS[way]
        axis = 1 - half if level < 2 else half
        if level == 0:
            src = pbuf.at[chunk, :, inner(way), far_lanes(half, 2)]
            dst = r1.at[chunk, half, :, inner(way), :]
        elif level == 1:
            src = pbuf.at[chunk, :, :, far_lanes(half, step)]
            dst = r2.at[chunk, half, way]
        elif level == 2:
            src = pbuf.at[chunk, :, inner(way), near_lanes(half, 2)]
            dst = r3.at[chunk, half, :, inner(way), :]
        else:
            src = pbuf.at[chunk, :, :, near_lanes(half, step)]
            dst = r4.at[chunk, half, way]
        index = level * 4 + half * 2 + way
        return remote(
            src, dst, p_send.at[chunk, index], p_recv.at[chunk, index], neighbour(axis, step)
        )

    def scatter_start(chunk, level):
        each(lambda half, way: scatter_copy(chunk, level, half, way).start())

    def mine(half):
        return lanes(half * WIDE + x * QUAD + z * HALF, HALF)

    def scatter_step(chunk, level):
        for half in (0, 1):
            for way in (0, 1):
                scatter_copy(chunk, level, half, way).wait_recv()
            if level % 2 == 0:
                for way in (0, 1):
                    cols = (far_lanes if level == 0 else near_lanes)(half, WAYS[way])
                    span = inner(way)
                    landed = (r1 if level == 0 else r3)[chunk, half, :, span, :]
                    total = wide(pbuf[chunk, :, span, cols]) + wide(landed)
                    pbuf[chunk, :, span, cols] = total.astype(jnp.bfloat16)
                    scatter_copy(chunk, level + 1, half, way).start()
            elif level == 1:
                cols = far_lanes(half, 0)
                total = (
                    wide(pbuf[chunk, :, :, cols])
                    + wide(r2[chunk, half, 0])
                    + wide(r2[chunk, half, 1])
                )
                pbuf[chunk, :, :, cols] = total.astype(jnp.bfloat16)
                for way in (0, 1):
                    scatter_copy(chunk, 2, half, way).start()
            else:
                total = (
                    wide(pbuf[chunk, :, :, near_lanes(half, 0)])
                    + wide(r4[chunk, half, 0])
                    + wide(r4[chunk, half, 1])
                )
                total = wide(xbuf[chunk, :, :, mine(half)]) + total
                span = pl.ds(pl.multiple_of(chunk * tall, tall), tall)
                out_ref[span, half * HALF : (half + 1) * HALF] = total.astype(
                    jnp.bfloat16
                ).reshape(tall, HALF)

    def scatter_sent(chunk, level):
        each(lambda half, way: scatter_copy(chunk, level, half, way).wait_send())

    first = 2 * (jnp.maximum(me - 8, 0) // 2)

    def mask():
        span = WINDOW * rows
        near = lanes((me // 2) * (2 * rows), 2 * rows)
        part = segment_ref[:, near].astype(jnp.float32)
        turned = jnp.transpose(jnp.broadcast_to(part, (2 * rows, 2 * rows)))
        query_seg = jnp.where(me % 2 == 1, turned[rows:], turned[:rows])[:, :1]
        key_seg = segment_ref[:, lanes(first * rows, span)].astype(jnp.float32)
        query_pos = me * rows + lax.broadcasted_iota(jnp.int32, (rows, span), 0)
        key_pos = first * rows + lax.broadcasted_iota(jnp.int32, (rows, span), 1)
        allowed = (key_pos <= query_pos) & (query_seg == key_seg)
        bias[...] = jnp.where(allowed, 0.0, -jnp.inf)

    def prefill(piece):
        @pl.loop(0, heads)
        def _(i):
            head = piece * heads + i

            def joined(base):
                cols = lanes(base + head * HD, HD)
                return jnp.concatenate(
                    [
                        pbuf[(first + b) // SIDE, (first + b) % SIDE, :, cols]
                        for b in range(WINDOW)
                    ],
                    axis=0,
                )

            keys, values = joined(0), joined(width)
            for j in range(group):
                cols = lanes((head * group + j) * HD, HD)
                scores = lax.dot_general(
                    query_ref[:, cols],
                    keys,
                    (((1,), (1,)), ((), ())),
                    preferred_element_type=jnp.float32,
                )
                scores = scores * scale + bias[...]
                top = jnp.max(scores, axis=-1, keepdims=True)
                weights = jnp.exp(scores - top).astype(jnp.bfloat16)
                total = jnp.sum(wide(weights), axis=-1, keepdims=True)
                summed = jnp.dot(weights, values, preferred_element_type=jnp.float32)
                to = pl.ds(pl.multiple_of(x * rows, rows), rows)
                abuf[to, cols] = (summed / total).astype(jnp.bfloat16)

    def decode():
        query = wide(incoming[0])
        for t in range(1, PEERS):
            query = query + wide(incoming[t])
        query = query.astype(jnp.bfloat16)
        count = 2 * tall

        def cached(base):
            return pbuf[0:2, :, :, WIDE + base : WIDE + base + HD].reshape(count, HD)

        owner = lax.broadcasted_iota(jnp.int32, (H, count), 0) // group
        scores = jnp.zeros((H, count), jnp.float32)
        for head in range(KVH):
            part = lax.dot_general(
                query,
                cached(head * HD),
                (((1,), (1,)), ((), ())),
                preferred_element_type=jnp.float32,
            )
            scores = jnp.where(owner == head, part, scores)
        visible = lax.broadcasted_iota(jnp.int32, (H, count), 1) < length_ref[0]
        scores = jnp.where(visible, scores * scale, -jnp.inf)
        top = jnp.max(scores, axis=-1, keepdims=True)
        weights = jnp.exp(scores - top).astype(jnp.bfloat16)
        total = jnp.sum(wide(weights), axis=-1, keepdims=True)
        owner = lax.broadcasted_iota(jnp.int32, (H, HD), 0) // group
        summed = jnp.zeros((H, HD), jnp.float32)
        for head in range(KVH):
            part = jnp.dot(
                weights, cached(width + head * HD), preferred_element_type=jnp.float32
            )
            summed = jnp.where(owner == head, part, summed)
        own[...] = summed / total

    def project(other):
        total = wide(rbuf[other]) + jnp.dot(
            abuf[...], wbuf[other], preferred_element_type=jnp.float32
        )
        value = total.astype(jnp.bfloat16)
        for half in (0, 1):
            to = lanes(half * WIDE + x * QUAD + other * HALF, HALF)
            part = value[:, half * HALF : (half + 1) * HALF]
            for chunk in range(SIDE):
                xbuf[chunk, z, :, to] = part[chunk * rows : (chunk + 1) * rows]
            xdec[:, to] = part[tall:]

    def scaled(read, owner, write):
        total = jnp.zeros((SUB, HALF), jnp.float32)
        for block in range(D // HALF):
            value = wide(read(slice(block * HALF, (block + 1) * HALF)))
            total = total + value * value
        inverse = lax.rsqrt(jnp.sum(total, axis=-1, keepdims=True) / D + epsilon)
        for block in range(D // HALF):
            cols = slice(block * HALF, (block + 1) * HALF)
            gain = gain_ref[3:4, cols]
            for k in (2, 1, 0):
                gain = jnp.where(owner == k, gain_ref[k : k + 1, cols], gain)
            write(cols, (wide(read(cols)) * inverse * gain).astype(jnp.bfloat16))

    def normalize(chunk):
        @pl.loop(0, tall // SUB)
        def _(t):
            per = rows // SUB
            span = pl.ds(pl.multiple_of((t % per) * SUB, SUB), SUB)
            to = pl.ds(pl.multiple_of(t * SUB, SUB), SUB)
            owner = tenant_ref[pl.ds(pl.multiple_of(chunk * tall + t * SUB, SUB), SUB), :]

            def write(cols, value):
                normed[to, cols] = value

            scaled(lambda cols: xbuf[chunk, t // per, span, cols], owner, write)

    def normalize_dec():
        def write(cols, value):
            normed[tall : tall + SUB, cols] = value

        owner = tenant_ref[PEERS * rows : PEERS * rows + SUB, :]
        scaled(lambda cols: xdec[:, cols], owner, write)

    def lift(tile, size):
        cols = slice(tile * size, (tile + 1) * size)
        gate = jnp.dot(normed[...], wg_ref[:, cols], preferred_element_type=jnp.float32)
        up = jnp.dot(normed[...], wu_ref[:, cols], preferred_element_type=jnp.float32)
        hidden[:, cols] = (gate / (1.0 + jnp.exp(-gate)) * up).astype(jnp.bfloat16)

    def lower(chunk):
        @pl.loop(0, D // QUAD)
        def _(tile):
            cols = lanes(tile * QUAD, QUAD)
            part = jnp.dot(hidden[...], wd_ref[:, cols], preferred_element_type=jnp.float32)
            part = part.astype(jnp.bfloat16)
            pbuf[chunk, :, :, cols] = part[:tall].reshape(SIDE, rows, QUAD)

            @pl.when(chunk == 0)
            def _():
                for i in range(SIDE):
                    @pl.when(tile < SIDE)
                    def _():
                        pdec[tile * SIDE + i, :, :HALF] = part[tall:, i * HALF : (i + 1) * HALF]

                    @pl.when(tile >= SIDE)
                    def _():
                        pdec[i * SIDE + tile - SIDE, :, HALF:] = part[
                            tall:, i * HALF : (i + 1) * HALF
                        ]

    barrier = pltpu.get_barrier_semaphore()

    @pl.loop(1, PEERS)
    def _(k):
        pl.semaphore_signal(barrier, inc=1, device_id={"tok": ahead(k)}, device_id_type=MESH)

    @pl.loop(1, groups)
    def _(k):
        pl.semaphore_signal(
            barrier, inc=1, device_id={"grp": lax.rem(grp + k, groups)}, device_id_type=MESH
        )

    fetch = pltpu.make_async_copy(cache_hbm, pbuf.at[0:2, :, :, pl.ds(WIDE, WIDE)], w_sem.at[0])
    fetch.start()
    fetch_wo = pltpu.make_async_copy(wo_hbm, wbuf.at[z], w_sem.at[4])
    fetch_wo.start()
    pbuf[z, x, :, 0:WIDE] = pair_ref[...]
    column[grp] = dec_ref[...]
    rbuf[z, 0:tall, :] = resid_ref[pl.ds(pl.multiple_of(z * tall, tall), tall), :]
    rbuf[z, tall : tall + SUB, :] = resid_ref[PEERS * rows : PEERS * rows + SUB, :]
    pl.semaphore_wait(barrier, PEERS + groups - 2)

    @pl.loop(1, groups)
    def _(k):
        group_copy(k, False).start()

    gather_start(k_args, 0, 0)
    for way in (0, 1):
        wz_copy(0, way, False).start()
    for piece in range(1, PIECES):
        gather_start(k_args, piece, 0)

    @pl.loop(0, PEERS)
    def _(t):
        tz, tx = t // SIDE, t % SIDE
        for half in (0, 1):
            source = lanes(t * BLOCK + half * HALF, HALF)
            inside = lanes(half * WIDE + tx * QUAD + tz * HALF, HALF)
            place = t * HALF if half == 0 else WIDE + tx * QUAD + tz * HALF
            target = lanes(place, HALF)
            pltpu.make_async_copy(wg_hbm.at[source, :], wg_ref.at[inside, :], w_sem.at[1]).start()
            pltpu.make_async_copy(wu_hbm.at[source, :], wu_ref.at[inside, :], w_sem.at[2]).start()
            pltpu.make_async_copy(wd_hbm.at[:, source], wd_ref.at[:, target], w_sem.at[3]).start()

    mask()

    @pl.loop(1, groups)
    def _(k):
        group_copy(k, True).wait_recv()

    @pl.loop(0, PEERS)
    def _(t):
        request = request_ref[grp * PEERS + t]
        row = column[request // PEERS]
        held = request % PEERS == me
        outgoing[t] = jnp.where(held, wide(row), 0.0).astype(jnp.bfloat16)

    @pl.loop(1, PEERS)
    def _(k):
        query_copy(k, False).start()

    incoming[me] = outgoing[me]

    for wave in range(PIECES + 3):
        for level in range(4):
            piece = wave - level
            if 0 <= piece < PIECES:
                gather_step(k_args, piece, level)
        if wave == 0:
            for way in (0, 1):
                wz_copy(0, way, True).wait_recv()
            for way in (0, 1):
                wz_copy(1, way, False).start()
            for other in (1, 3):
                for way in (0, 1):
                    wy_copy(other, 0, way, False).start()
                wc_copy(other, 0, False).start()
            for k in (1, 2, 3):
                for copy in base_copies(k, False):
                    copy.start()
        if wave == 1:
            for way in (0, 1):
                wz_copy(1, way, True).wait_recv()
            for way in (0, 1):
                wy_copy(2, 0, way, False).start()
            wc_copy(2, 0, False).start()
        if wave == 2:
            fetch.wait()

            @pl.loop(1, PEERS)
            def _(k):
                query_copy(k, True).wait_recv()

            decode()

            @pl.loop(1, PEERS)
            def _(k):
                dec_copy(k, False).start()

            dbuf[me] = own[...]
        if wave >= 3:
            prefill(wave - 3)
            for way in (0, 1):
                a_copy(wave - 3, 0, way, False).start()
        if wave >= 4:
            for way in (0, 1):
                a_copy(wave - 4, 0, way, True).wait_recv()
                a_copy(wave - 4, 1, way, False).start()
        if wave == 4:
            for other in (1, 3, 2):
                for way in (0, 1):
                    wy_copy(other, 0, way, True).wait_recv()
                    wy_copy(other, 1, way, False).start()
                    wc_copy(other, -WAYS[way], False).start()

    for way in (0, 1):
        a_copy(PIECES - 1, 0, way, True).wait_recv()
        a_copy(PIECES - 1, 1, way, False).start()

    @pl.loop(1, PEERS)
    def _(k):
        dec_copy(k, True).wait_recv()

    for head in range(H):
        abuf[tall : tall + SUB, head * HD : (head + 1) * HD] = dbuf[:, head, :].astype(
            jnp.bfloat16
        )
    for other in (1, 3, 2):
        for way in (0, 1):
            wy_copy(other, 1, way, True).wait_recv()
        wc_copy(other, 2, False).start()
    for k in (1, 2, 3):
        for copy in base_copies(k, True):
            copy.wait_recv()
    for piece in range(PIECES):
        for way in (0, 1):
            a_copy(piece, 1, way, True).wait_recv()
    for other in (1, 2, 3):
        for offset in (-1, 0, 1, 2):
            wc_copy(other, offset, True).wait_recv()
    fetch_wo.wait()

    @pl.loop(0, SIDE)
    def _(other):
        project(other)

    for k in (1, 2, 3):
        for copy in xdec_copies(k, False):
            copy.start()

    @pl.loop(0, SIDE)
    def _(chunk):
        gather_start(x_args, chunk, 0)

    @pl.loop(0, PIECES)
    def _(piece):
        for level in range(4):
            gather_sent(k_args, piece, level)

    gather_step(x_args, 0, 0)
    gather_step(x_args, 0, 1)
    size = 256

    @pl.loop(0, SIDE + 2)
    def _(s):
        x_on = s < SIDE
        next_on = s < SIDE - 1
        f_on = jnp.logical_and(s >= 1, s < SIDE + 1)
        p_on = s >= 2

        @pl.when(s == 1)
        def _():
            pltpu.make_async_copy(wg_ref, wg_ref, w_sem.at[1]).wait()
            pltpu.make_async_copy(wu_ref, wu_ref, w_sem.at[2]).wait()
            pltpu.make_async_copy(wd_ref, wd_ref, w_sem.at[3]).wait()
            for k in (1, 2, 3):
                for copy in xdec_copies(k, True):
                    copy.wait_recv()
            normalize_dec()

        @pl.when(f_on)
        def _():
            normalize(s - 1)

        @pl.when(x_on)
        def _():
            gather_step(x_args, s, 2)

        @pl.when(next_on)
        def _():
            gather_step(x_args, s + 1, 0)

        @pl.when(p_on)
        def _():
            scatter_step(s - 2, 0)

        @pl.when(f_on)
        def _():
            lift(0, size)

        @pl.when(next_on)
        def _():
            gather_step(x_args, s + 1, 1)

        @pl.when(p_on)
        def _():
            scatter_step(s - 2, 1)

        @pl.when(f_on)
        def _():
            for tile in range(1, ffw // size):
                lift(tile, size)

        @pl.when(p_on)
        def _():
            scatter_step(s - 2, 2)

        @pl.when(f_on)
        def _():
            lower(s - 1)
            scatter_start(s - 1, 0)

        @pl.when(s == 1)
        def _():
            @pl.loop(1, PEERS)
            def _(k):
                fdec_copy(k, False).start()

        @pl.when(x_on)
        def _():
            gather_step(x_args, s, 3)

        @pl.when(p_on)
        def _():
            scatter_step(s - 2, 3)

    @pl.loop(1, PEERS)
    def _(k):
        fdec_copy(k, True).wait_recv()

    rdec[me] = pdec[me]
    total = wide(rdec[0])
    for t in range(1, PEERS):
        total = total + wide(rdec[t])
    for half in (0, 1):
        part = wide(xdec[:, mine(half)]) + total[:, half * HALF : (half + 1) * HALF]
        out_ref[PEERS * rows : PEERS * rows + SUB, half * HALF : (half + 1) * HALF] = part.astype(
            jnp.bfloat16
        )

    @pl.loop(1, groups)
    def _(k):
        group_copy(k, False).wait_send()

    @pl.loop(1, PEERS)
    def _(k):
        query_copy(k, False).wait_send()
        dec_copy(k, False).wait_send()
        fdec_copy(k, False).wait_send()

    for way in (0, 1):
        for level in (0, 1):
            wz_copy(level, way, False).wait_send()
            for other in (1, 2, 3):
                wy_copy(other, level, way, False).wait_send()
            for piece in range(PIECES):
                a_copy(piece, level, way, False).wait_send()
    for other in (1, 2, 3):
        for offset in (-1, 0, 1, 2):
            wc_copy(other, offset, False).wait_send()
        for copy in base_copies(other, False) + tuple(xdec_copies(other, False)):
            copy.wait_send()

    @pl.loop(0, SIDE)
    def _(chunk):
        for level in range(4):
            gather_sent(x_args, chunk, level)
            scatter_sent(chunk, level)


def layer_call(length, request, queries, pairs, segment, dec, cache, resid, owner, gains, *weights):
    wo, w_gate, w_up, w_down = weights
    rows = queries.shape[0]
    tall = SIDE * rows
    ffw = w_gate.shape[1]
    groups = lax.axis_size("grp")
    vmem = pl.BlockSpec(memory_space=pltpu.VMEM)
    smem = pl.BlockSpec(memory_space=pltpu.SMEM)
    hbm = pl.BlockSpec(memory_space=pl.ANY)
    bf16 = jnp.bfloat16
    dma = pltpu.SemaphoreType.DMA
    pairs_of = lambda *shape: [dma(shape), dma(shape)]
    return pl.pallas_call(
        layer_kernel,
        out_shape=jax.ShapeDtypeStruct(resid.shape, bf16),
        in_specs=[smem, smem, vmem, vmem, vmem, vmem, hbm, vmem, vmem, vmem] + [hbm] * 4,
        out_specs=vmem,
        scratch_shapes=[
            pltpu.VMEM((tall + SUB, D), bf16),
            pltpu.VMEM((SIDE, D, BLOCK), bf16),
            pltpu.VMEM((SIDE, SIDE, rows, D), bf16),
            pltpu.VMEM((SIDE, SIDE, rows, D), bf16),
            pltpu.VMEM((tall + SUB, D), bf16),
            pltpu.VMEM((tall + SUB, ffw), bf16),
            pltpu.VMEM((SIDE, 2, SIDE, rows, QUAD), bf16),
            pltpu.VMEM((SIDE, 2, 2, SIDE, rows, QUAD), bf16),
            pltpu.VMEM((SIDE, 2, SIDE, rows, HALF), bf16),
            pltpu.VMEM((SIDE, 2, 2, SIDE, rows, HALF), bf16),
            pltpu.VMEM(w_gate.shape, bf16),
            pltpu.VMEM(w_up.shape, bf16),
            pltpu.VMEM(w_down.shape, bf16),
            pltpu.VMEM((rows, WINDOW * rows), jnp.float32),
            pltpu.VMEM((groups, H, HD), bf16),
            pltpu.VMEM((PEERS, H, HD), bf16),
            pltpu.VMEM((PEERS, H, HD), bf16),
            pltpu.VMEM((H, HD), jnp.float32),
            pltpu.VMEM((PEERS, H, HD), jnp.float32),
            pltpu.VMEM((SIDE, tall + SUB, BLOCK), bf16),
            pltpu.VMEM((SUB, D), bf16),
            pltpu.VMEM((PEERS, SUB, BLOCK), bf16),
            pltpu.VMEM((PEERS, SUB, BLOCK), bf16),
            dma((5,)),
            *pairs_of(PIECES, 16),
            *pairs_of(groups),
            *pairs_of(PEERS),
            *pairs_of(PEERS),
            *pairs_of(PIECES, 4),
            *pairs_of(4),
            *pairs_of(12),
            *pairs_of(12),
            *pairs_of(8),
            *pairs_of(8),
            *pairs_of(SIDE, 16),
            *pairs_of(SIDE, 16),
            *pairs_of(PEERS),
        ],
        compiler_params=pltpu.CompilerParams(
            collective_id=1, has_side_effects=True, vmem_limit_bytes=67043328
        ),
        name="layer",
    )(length, request, queries, pairs, segment, dec, cache, resid, owner, gains, *weights)


def shards(
    pre_q,
    pre_kv,
    pre_segment,
    dec_q,
    cache,
    cache_len,
    slot_request,
    resid,
    wo,
    tenant,
    norm_gain,
    w_gate,
    w_up,
    w_down,
):
    rows = pre_q.shape[0]
    tokens, cols = resid.shape
    split = resid.reshape(PEERS, rows + 1, cols)
    natural = jnp.concatenate([split[:, :rows].reshape(PEERS * rows, cols), split[:, rows]], axis=0)
    owner = tenant[0].reshape(PEERS, rows + 1)
    main = jnp.swapaxes(owner[:, :rows].reshape(SIDE, SIDE, rows), 0, 1).reshape(PEERS * rows)
    owner = jnp.concatenate([main, owner[:, rows]], axis=0)
    owner = jnp.broadcast_to(owner[:, None], (tokens, HALF))
    gains = norm_gain.reshape(-1, SIDE, SIDE, 2, HALF).transpose(0, 3, 2, 1, 4).reshape(-1, D)
    result = layer_call(
        cache_len,
        slot_request,
        pre_q,
        pre_kv,
        pre_segment,
        dec_q.reshape(H, HD),
        cache.reshape(2, SIDE, -1, cache.shape[2]),
        natural,
        owner,
        gains,
        wo,
        w_gate,
        w_up,
        w_down,
    )
    main = result[: PEERS * rows].reshape(SIDE, SIDE, rows, cols)
    main = jnp.swapaxes(main, 0, 1).reshape(PEERS, rows, cols)
    last = result[PEERS * rows :].reshape(PEERS, 1, cols)
    return jnp.concatenate([main, last], axis=1).reshape(tokens, cols)


def solution(mesh):
    in_specs = (
        P(("grp", "tok"), None),
        P(("grp", "tok"), None),
        P("grp", None),
        P(("grp", "tok"), None),
        P(("grp", "tok"), None, None),
        P(("grp", "tok")),
        P(),
        P("grp", "tok"),
        P(None, "tok"),
        P("grp", None),
        P(),
        P(None, "tok"),
        P(None, "tok"),
        P("tok", None),
    )
    out_specs = P("grp", "tok")
    return jax.shard_map(shards, mesh=mesh, in_specs=in_specs, out_specs=out_specs, check_vma=False)
```

time: 469 us -> 209 us (0.45)
  waiting for transfers between devices: 363 us -> 0 us
  Pallas kernels: 0 us -> 201 us
  matrix products: 55.2 us -> 0 us
  local copies, waits for them, and re-layouts: 21.7 us -> 5.57 us
  between operations: 15.9 us -> 0.78 us
  starting transfers between devices: 5.6 us -> 0 us
  other arithmetic: 6.54 us -> 1.55 us
    all_gather x4 -> x0, waiting for transfers between devices: 260 us -> none  [the longest x1 76.7 us: shards(): piece = lax.all_gather(normed_part, 'tok', axis=1, tiled=True)]
    pallas_call x0 -> x1, Pallas kernels: none -> 201 us  [layer_call(): pl.pallas_call(layer_kernel, out_shape=jax.ShapeDtypeStruct(resid.shape,...]
    reduce_scatter x1 -> x0, waiting for transfers between devices: 94.2 us -> none  [shards(): lax.psum_scatter(lax.dot_general(w_down, hidden, (((0,), (1,)), ((), ()))...]
    dot_general x7 -> x0, matrix products: 53.5 us -> none  [the longest x1 26.3 us: shards(): lax.dot_general(w_down, hidden, (((0,), (1,)), ((), ())), preferred_eleme...]
    unnamed x13 -> x9, local copies, waits for them, and re-layouts: 11.9 us -> 0.15 us
    all_to_all x1 -> x0, waiting for transfers between devices: 7.6 us -> none  [copy_for_each(): return lax.all_to_all(copies, axis, split_axis=0, concat_axis=0, tiled=True)]
    all_to_all x1 -> x0, starting transfers between devices: 5.25 us -> none  [copy_for_each(): return lax.all_to_all(copies, axis, split_axis=0, concat_axis=0, tiled=True)]
  transfers between devices with their start and end apart: 6 -> 0, of which waited for: 6 -> 0; matrix products, arithmetic and copies ran while one was open for 2% -> 0% of each run, Pallas kernels for 0% -> 0%
where the time goes in v3:
time: 209 us
  Pallas kernels  201 us (96%)
  local copies, waits for them, and re-layouts  5.57 us (3%)
    pallas_call x1, Pallas kernels, layer_call(): pl.pallas_call(layer_kernel, out_shape=jax.ShapeDtypeStruct(resid.shape,...  201 us

profile of v3, /device:TPU:0, one launch (start us, length us, event | category | flops | bytes accessed | tf_op | source)
XLA Modules:
  0.0 209.1 jit_solution(6039258546766704837)
XLA Ops:
  0.0 1.2 reshape.39
  1.2 0.0 copy-start.3
  1.2 0.0 copy-start.1
  1.3 0.0 copy-start.2
  1.3 0.8 pad_maximum_fusion.1.resid_ref
  2.2 0.0 copy-done.3
  2.2 0.1 reshape_squeeze.3
  2.3 0.1 reshape.42
  2.4 0.2 slice_reduce_fusion
  2.6 1.0 broadcast_in_dim.2.tenant_ref
  3.6 0.0 copy-done.1
  3.6 0.1 reshape.43
  3.7 0.7 reshape.44.gain_ref
  4.3 0.0 copy-done.2
  4.3 0.6 reduce
  5.6 201.2 %layer.1 = bf16[1040,256]{1,0:T(8,128)(2,1)} custom-call(s32[1]{0:T(128)S(6)} %copy.38.length_ref, s32[128]{0:T(128)} %request_ref.1, bf16[64,4096]{1,0:T(8,128)(2,1)} %query_ref.1, bf16[64,2048]{1,0:T(8,128)(2,1)} %pair_ref.1, s32[1,1024]{1,0:T(1,128)} %segment_ref.1, bf16[32,128]{1,0:T(8,128)(2,1)} %bitcast.25, bf16[2,4,64,2048]{3,2,1,0:T(8,128)(2,1)} %bitcast.22, ...), custom_call_target="tpu_custom_call" | custom-call | tf_op jit(solution)/shard_map/layer/pallas_call | solution.py:813
  206.8 0.0 slice-start
  206.8 0.0 copy-start
  206.8 1.0 slice-done
  207.9 0.1 copy-done
  208.1 1.0 reshape.48
  (11 shorter events, 0.2 us)
Async XLA Ops:
  1.2 1.0 copy-start.3
  1.2 2.3 %copy-start.1 = (f32[4,4096]{1,0:T(4,128)S(1)}, f32[4,4096]{1,0:T(4,128)}, u32[]{:S(2)}) copy-start(f32[4,4096]{1,0:T(4,128)} %param.24) | copy-start | bytes 196612
  1.3 3.0 %copy-start.2 = (bf16[1,4096]{1,0:T(2,128)(2,1)S(1)}, bf16[1,4096]{1,0:T(2,128)(2,1)}, u32[]{:S(2)}) copy-start(bf16[1,4096]{1,0:T(2,128)(2,1)} %param.17) | copy-start | bytes 24580
  206.8 1.0 slice-start
  206.8 1.2 copy-start

commit v4 on v3

--- a/solution.py
+++ b/solution.py
@@ -20,6 +20,8 @@
 QUAD = SIDE * HALF
 SUB = 16
 PIECES = 4
+CHUNKS = 8
+PARTS = CHUNKS // SIDE
 WINDOW = 10
 CORES = 2
 
@@ -31,19 +33,22 @@
 def layer_kernel(
     length_ref,
     request_ref,
-    query_ref,
-    pair_ref,
+    query_hbm,
+    pair_hbm,
     segment_ref,
     dec_ref,
     cache_hbm,
-    resid_ref,
+    resid_hbm,
     tenant_ref,
-    gain_ref,
+    gain_hbm,
     wo_hbm,
     wg_hbm,
     wu_hbm,
     wd_hbm,
-    out_ref,
+    out_hbm,
+    qbuf,
+    gbuf,
+    obuf,
     abuf,
     wbuf,
     xbuf,
@@ -58,6 +63,7 @@
     wu_ref,
     wd_ref,
     bias,
+    tbuf,
     column,
     outgoing,
     incoming,
@@ -68,6 +74,7 @@
     pdec,
     rdec,
     w_sem,
+    o_sem,
     k_send,
     k_recv,
     g_send,
@@ -100,8 +107,10 @@
     groups = column.shape[0]
     z, x = me // SIDE, me % SIDE
     y, core = grp // CORES, grp % CORES
-    rows = query_ref.shape[0]
+    rows = query_hbm.shape[0]
     tall = SIDE * rows
+    part_rows = rows // PARTS
+    high = SIDE * part_rows
     width = KVH * HD
     group = H // KVH
     heads = KVH // PIECES
@@ -151,8 +160,19 @@
             return pbuf.at[hop(z, offset), :, span, cols]
         return pbuf.at[:, hop(x, offset), span, cols]
 
-    def x_block(chunk, half, offset, level, part):
-        span = inner(part)
+    def within(chunk, part=None):
+        base = (chunk % PARTS) * part_rows
+        if part is None:
+            return pl.ds(pl.multiple_of(base, SUB), part_rows)
+        count = part_rows // 2
+        return pl.ds(pl.multiple_of(base + part * count, SUB), count)
+
+    def half_of(part):
+        return pl.ds(part * (part_rows // 2), part_rows // 2)
+
+    def x_block(number, half, offset, level, part):
+        span = within(number, part)
+        chunk = number // PARTS
         if level < 2:
             if half == 0:
                 return xbuf.at[chunk, z, span, lanes(hop(x, offset) * QUAD, QUAD)]
@@ -240,7 +260,7 @@
     def group_copy(k, arriving):
         source = lax.rem(grp - k + groups, groups) if arriving else grp
         peer = {"grp": lax.rem(grp + k, groups)}
-        return remote(dec_ref, column.at[source], g_send.at[k], g_recv.at[k], peer)
+        return remote(column.at[grp], column.at[source], g_send.at[k], g_recv.at[k], peer)
 
     def ahead(k):
         return lax.rem(me + k, PEERS)
@@ -268,14 +288,14 @@
         last = pl.ds(PEERS * rows, PEERS)
         return (
             remote(
-                resid_ref.at[start, :],
+                resid_hbm.at[start, :],
                 rbuf.at[slot, pl.ds(0, tall), :],
                 b_send.at[2 * k],
                 b_recv.at[2 * k],
                 peer,
             ),
             remote(
-                resid_ref.at[last, :],
+                resid_hbm.at[last, :],
                 rbuf.at[slot, pl.ds(tall, PEERS), :],
                 b_send.at[2 * k + 1],
                 b_recv.at[2 * k + 1],
@@ -303,24 +323,25 @@
             return lanes(hop(z, offset) * QUAD, QUAD)
         return lanes(WIDE + hop(x, offset) * QUAD, QUAD)
 
-    def scatter_copy(chunk, level, half, way):
+    def scatter_copy(number, level, half, way):
         step = WAYS[way]
         axis = 1 - half if level < 2 else half
+        chunk, span = number // PARTS, within(number)
         if level == 0:
-            src = pbuf.at[chunk, :, inner(way), far_lanes(half, 2)]
-            dst = r1.at[chunk, half, :, inner(way), :]
+            src = pbuf.at[chunk, :, within(number, way), far_lanes(half, 2)]
+            dst = r1.at[number, half, :, half_of(way), :]
         elif level == 1:
-            src = pbuf.at[chunk, :, :, far_lanes(half, step)]
-            dst = r2.at[chunk, half, way]
+            src = pbuf.at[chunk, :, span, far_lanes(half, step)]
+            dst = r2.at[number, half, way]
         elif level == 2:
-            src = pbuf.at[chunk, :, inner(way), near_lanes(half, 2)]
-            dst = r3.at[chunk, half, :, inner(way), :]
+            src = pbuf.at[chunk, :, within(number, way), near_lanes(half, 2)]
+            dst = r3.at[number, half, :, half_of(way), :]
         else:
-            src = pbuf.at[chunk, :, :, near_lanes(half, step)]
-            dst = r4.at[chunk, half, way]
+            src = pbuf.at[chunk, :, span, near_lanes(half, step)]
+            dst = r4.at[number, half, way]
         index = level * 4 + half * 2 + way
         return remote(
-            src, dst, p_send.at[chunk, index], p_recv.at[chunk, index], neighbour(axis, step)
+            src, dst, p_send.at[number, index], p_recv.at[number, index], neighbour(axis, step)
         )
 
     def scatter_start(chunk, level):
@@ -329,39 +350,46 @@
     def mine(half):
         return lanes(half * WIDE + x * QUAD + z * HALF, HALF)
 
-    def scatter_step(chunk, level):
+    def out_copy(number):
+        span = pl.ds(pl.multiple_of(number * high, high), high)
+        return pltpu.make_async_copy(obuf.at[span, :], out_hbm.at[span, :], o_sem.at[number])
+
+    def scatter_step(number, level):
+        chunk, span = number // PARTS, within(number)
         for half in (0, 1):
             for way in (0, 1):
-                scatter_copy(chunk, level, half, way).wait_recv()
+                scatter_copy(number, level, half, way).wait_recv()
             if level % 2 == 0:
                 for way in (0, 1):
                     cols = (far_lanes if level == 0 else near_lanes)(half, WAYS[way])
-                    span = inner(way)
-                    landed = (r1 if level == 0 else r3)[chunk, half, :, span, :]
-                    total = wide(pbuf[chunk, :, span, cols]) + wide(landed)
-                    pbuf[chunk, :, span, cols] = total.astype(jnp.bfloat16)
-                    scatter_copy(chunk, level + 1, half, way).start()
+                    some = within(number, way)
+                    landed = (r1 if level == 0 else r3)[number, half, :, half_of(way), :]
+                    total = wide(pbuf[chunk, :, some, cols]) + wide(landed)
+                    pbuf[chunk, :, some, cols] = total.astype(jnp.bfloat16)
+                    scatter_copy(number, level + 1, half, way).start()
             elif level == 1:
                 cols = far_lanes(half, 0)
                 total = (
-                    wide(pbuf[chunk, :, :, cols])
-                    + wide(r2[chunk, half, 0])
-                    + wide(r2[chunk, half, 1])
+                    wide(pbuf[chunk, :, span, cols])
+                    + wide(r2[number, half, 0])
+                    + wide(r2[number, half, 1])
                 )
-                pbuf[chunk, :, :, cols] = total.astype(jnp.bfloat16)
+                pbuf[chunk, :, span, cols] = total.astype(jnp.bfloat16)
                 for way in (0, 1):
-                    scatter_copy(chunk, 2, half, way).start()
+                    scatter_copy(number, 2, half, way).start()
             else:
                 total = (
-                    wide(pbuf[chunk, :, :, near_lanes(half, 0)])
-                    + wide(r4[chunk, half, 0])
-                    + wide(r4[chunk, half, 1])
+                    wide(pbuf[chunk, :, span, near_lanes(half, 0)])
+                    + wide(r4[number, half, 0])
+                    + wide(r4[number, half, 1])
                 )
-                total = wide(xbuf[chunk, :, :, mine(half)]) + total
-                span = pl.ds(pl.multiple_of(chunk * tall, tall), tall)
-                out_ref[span, half * HALF : (half + 1) * HALF] = total.astype(
-                    jnp.bfloat16
-                ).reshape(tall, HALF)
+                total = wide(xbuf[chunk, :, span, mine(half)]) + total
+                to = pl.ds(pl.multiple_of(number * high, high), high)
+                obuf[to, half * HALF : (half + 1) * HALF] = total.astype(jnp.bfloat16).reshape(
+                    high, HALF
+                )
+        if level == 3:
+            out_copy(number).start()
 
     def scatter_sent(chunk, level):
         each(lambda half, way: scatter_copy(chunk, level, half, way).wait_send())
@@ -399,7 +427,7 @@
             for j in range(group):
                 cols = lanes((head * group + j) * HD, HD)
                 scores = lax.dot_general(
-                    query_ref[:, cols],
+                    qbuf[:, cols],
                     keys,
                     (((1,), (1,)), ((), ())),
                     preferred_element_type=jnp.float32,
@@ -466,30 +494,36 @@
         inverse = lax.rsqrt(jnp.sum(total, axis=-1, keepdims=True) / D + epsilon)
         for block in range(D // HALF):
             cols = slice(block * HALF, (block + 1) * HALF)
-            gain = gain_ref[3:4, cols]
+            gain = gbuf[3:4, cols]
             for k in (2, 1, 0):
-                gain = jnp.where(owner == k, gain_ref[k : k + 1, cols], gain)
+                gain = jnp.where(owner == k, gbuf[k : k + 1, cols], gain)
             write(cols, (wide(read(cols)) * inverse * gain).astype(jnp.bfloat16))
 
-    def normalize(chunk):
-        @pl.loop(0, tall // SUB)
+    def owners(base):
+        part = tenant_ref[:, lanes(base, HALF)].astype(jnp.float32)
+        return jnp.transpose(jnp.broadcast_to(part, (HALF, HALF)))
+
+    def normalize(number):
+        chunk = number // PARTS
+        tbuf[...] = owners(number * high)
+
+        @pl.loop(0, high // SUB)
         def _(t):
-            per = rows // SUB
-            span = pl.ds(pl.multiple_of((t % per) * SUB, SUB), SUB)
+            per = part_rows // SUB
+            base = (number % PARTS) * part_rows + (t % per) * SUB
+            span = pl.ds(pl.multiple_of(base, SUB), SUB)
             to = pl.ds(pl.multiple_of(t * SUB, SUB), SUB)
-            owner = tenant_ref[pl.ds(pl.multiple_of(chunk * tall + t * SUB, SUB), SUB), :]
 
             def write(cols, value):
                 normed[to, cols] = value
 
-            scaled(lambda cols: xbuf[chunk, t // per, span, cols], owner, write)
+            scaled(lambda cols: xbuf[chunk, t // per, span, cols], tbuf[to, :], write)
 
     def normalize_dec():
         def write(cols, value):
-            normed[tall : tall + SUB, cols] = value
-
-        owner = tenant_ref[PEERS * rows : PEERS * rows + SUB, :]
-        scaled(lambda cols: xdec[:, cols], owner, write)
+            normed[high : high + SUB, cols] = value
+
+        scaled(lambda cols: xdec[:, cols], owners(PEERS * rows)[:SUB], write)
 
     def lift(tile, size):
         cols = slice(tile * size, (tile + 1) * size)
@@ -497,26 +531,28 @@
         up = jnp.dot(normed[...], wu_ref[:, cols], preferred_element_type=jnp.float32)
         hidden[:, cols] = (gate / (1.0 + jnp.exp(-gate)) * up).astype(jnp.bfloat16)
 
-    def lower(chunk):
+    def lower(number):
         @pl.loop(0, D // QUAD)
         def _(tile):
             cols = lanes(tile * QUAD, QUAD)
             part = jnp.dot(hidden[...], wd_ref[:, cols], preferred_element_type=jnp.float32)
             part = part.astype(jnp.bfloat16)
-            pbuf[chunk, :, :, cols] = part[:tall].reshape(SIDE, rows, QUAD)
-
-            @pl.when(chunk == 0)
+            pbuf[number // PARTS, :, within(number), cols] = part[:high].reshape(
+                SIDE, part_rows, QUAD
+            )
+
+            @pl.when(number == 0)
             def _():
                 for i in range(SIDE):
+                    piece = part[high:, i * HALF : (i + 1) * HALF]
+
                     @pl.when(tile < SIDE)
                     def _():
-                        pdec[tile * SIDE + i, :, :HALF] = part[tall:, i * HALF : (i + 1) * HALF]
+                        pdec[tile * SIDE + i, :, :HALF] = piece
 
                     @pl.when(tile >= SIDE)
                     def _():
-                        pdec[i * SIDE + tile - SIDE, :, HALF:] = part[
-                            tall:, i * HALF : (i + 1) * HALF
-                        ]
+                        pdec[i * SIDE + tile - SIDE, :, HALF:] = piece
 
     barrier = pltpu.get_barrier_semaphore()
 
@@ -530,25 +566,108 @@
             barrier, inc=1, device_id={"grp": lax.rem(grp + k, groups)}, device_id_type=MESH
         )
 
-    fetch = pltpu.make_async_copy(cache_hbm, pbuf.at[0:2, :, :, pl.ds(WIDE, WIDE)], w_sem.at[0])
-    fetch.start()
-    fetch_wo = pltpu.make_async_copy(wo_hbm, wbuf.at[z], w_sem.at[4])
-    fetch_wo.start()
-    pbuf[z, x, :, 0:WIDE] = pair_ref[...]
-    column[grp] = dec_ref[...]
-    rbuf[z, 0:tall, :] = resid_ref[pl.ds(pl.multiple_of(z * tall, tall), tall), :]
-    rbuf[z, tall : tall + SUB, :] = resid_ref[PEERS * rows : PEERS * rows + SUB, :]
+    def local(src, dst, index):
+        copy = pltpu.make_async_copy(src, dst, w_sem.at[index])
+        copy.start()
+        return copy
+
+    fetch_pair = local(pair_hbm, pbuf.at[z, x, :, pl.ds(0, WIDE)], 5)
+    fetch_query = local(query_hbm, qbuf, 6)
+    fetch = local(cache_hbm, pbuf.at[0:2, :, :, pl.ds(WIDE, WIDE)], 0)
+    for head in range(H):
+        own[head : head + 1, :] = wide(dec_ref[:, head * HD : (head + 1) * HD])
+    column[grp] = own[...].astype(jnp.bfloat16)
+    fetch_pair.wait()
     pl.semaphore_wait(barrier, PEERS + groups - 2)
 
     @pl.loop(1, groups)
     def _(k):
         group_copy(k, False).start()
 
-    gather_start(k_args, 0, 0)
+    for piece in range(PIECES):
+        gather_start(k_args, piece, 0)
     for way in (0, 1):
         wz_copy(0, way, False).start()
-    for piece in range(1, PIECES):
-        gather_start(k_args, piece, 0)
+    fetch_wo = local(wo_hbm, wbuf.at[z], 4)
+    fetch_gain = local(gain_hbm, gbuf, 7)
+    tall_at = pl.ds(pl.multiple_of(z * tall, tall), tall)
+    last_at = pl.ds(PEERS * rows, PEERS)
+    fetch_base = local(resid_hbm.at[tall_at, :], rbuf.at[z, pl.ds(0, tall), :], 8)
+    fetch_last = local(resid_hbm.at[last_at, :], rbuf.at[z, pl.ds(tall, PEERS), :], 9)
+    mask()
+    near_order = ((0, 0), (1, 0), (0, 1), (2, 0), (1, 1), (3, 0), (2, 1), (3, 1))
+    for piece, level in near_order:
+        gather_step(k_args, piece, level)
+
+    @pl.loop(1, groups)
+    def _(k):
+        group_copy(k, True).wait_recv()
+
+    @pl.loop(0, PEERS)
+    def _(t):
+        request = request_ref[grp * PEERS + t]
+        row = column[request // PEERS]
+        held = request % PEERS == me
+        outgoing[t] = jnp.where(held, wide(row), 0.0).astype(jnp.bfloat16)
+
+    @pl.loop(1, PEERS)
+    def _(k):
+        query_copy(k, False).start()
+
+    incoming[me] = outgoing[me]
+    fetch_query.wait()
+
+    def attend(piece):
+        gather_step(k_args, piece, 3)
+        prefill(piece)
+        for way in (0, 1):
+            a_copy(piece, 0, way, False).start()
+
+    def pass_on(piece):
+        for way in (0, 1):
+            a_copy(piece, 0, way, True).wait_recv()
+            a_copy(piece, 1, way, False).start()
+
+    gather_step(k_args, 0, 2)
+    for way in (0, 1):
+        wz_copy(0, way, True).wait_recv()
+    for way in (0, 1):
+        wz_copy(1, way, False).start()
+    for other in (1, 3):
+        for way in (0, 1):
+            wy_copy(other, 0, way, False).start()
+        wc_copy(other, 0, False).start()
+    gather_step(k_args, 1, 2)
+    attend(0)
+    for way in (0, 1):
+        wz_copy(1, way, True).wait_recv()
+    for way in (0, 1):
+        wy_copy(2, 0, way, False).start()
+    wc_copy(2, 0, False).start()
+    gather_step(k_args, 2, 2)
+    attend(1)
+    pass_on(0)
+    gather_step(k_args, 3, 2)
+    for k in (1, 2, 3):
+        for copy in base_copies(k, False):
+            copy.start()
+    attend(2)
+    pass_on(1)
+    fetch.wait()
+
+    @pl.loop(1, PEERS)
+    def _(k):
+        query_copy(k, True).wait_recv()
+
+    decode()
+
+    @pl.loop(1, PEERS)
+    def _(k):
+        dec_copy(k, False).start()
+
+    dbuf[me] = own[...]
+    attend(3)
+    pass_on(2)
 
     @pl.loop(0, PEERS)
     def _(t):
@@ -562,80 +681,12 @@
             pltpu.make_async_copy(wu_hbm.at[source, :], wu_ref.at[inside, :], w_sem.at[2]).start()
             pltpu.make_async_copy(wd_hbm.at[:, source], wd_ref.at[:, target], w_sem.at[3]).start()
 
-    mask()
-
-    @pl.loop(1, groups)
-    def _(k):
-        group_copy(k, True).wait_recv()
-
-    @pl.loop(0, PEERS)
-    def _(t):
-        request = request_ref[grp * PEERS + t]
-        row = column[request // PEERS]
-        held = request % PEERS == me
-        outgoing[t] = jnp.where(held, wide(row), 0.0).astype(jnp.bfloat16)
-
-    @pl.loop(1, PEERS)
-    def _(k):
-        query_copy(k, False).start()
-
-    incoming[me] = outgoing[me]
-
-    for wave in range(PIECES + 3):
-        for level in range(4):
-            piece = wave - level
-            if 0 <= piece < PIECES:
-                gather_step(k_args, piece, level)
-        if wave == 0:
-            for way in (0, 1):
-                wz_copy(0, way, True).wait_recv()
-            for way in (0, 1):
-                wz_copy(1, way, False).start()
-            for other in (1, 3):
-                for way in (0, 1):
-                    wy_copy(other, 0, way, False).start()
-                wc_copy(other, 0, False).start()
-            for k in (1, 2, 3):
-                for copy in base_copies(k, False):
-                    copy.start()
-        if wave == 1:
-            for way in (0, 1):
-                wz_copy(1, way, True).wait_recv()
-            for way in (0, 1):
-                wy_copy(2, 0, way, False).start()
-            wc_copy(2, 0, False).start()
-        if wave == 2:
-            fetch.wait()
-
-            @pl.loop(1, PEERS)
-            def _(k):
-                query_copy(k, True).wait_recv()
-
-            decode()
-
-            @pl.loop(1, PEERS)
-            def _(k):
-                dec_copy(k, False).start()
-
-            dbuf[me] = own[...]
-        if wave >= 3:
-            prefill(wave - 3)
-            for way in (0, 1):
-                a_copy(wave - 3, 0, way, False).start()
-        if wave >= 4:
-            for way in (0, 1):
-                a_copy(wave - 4, 0, way, True).wait_recv()
-                a_copy(wave - 4, 1, way, False).start()
-        if wave == 4:
-            for other in (1, 3, 2):
-                for way in (0, 1):
-                    wy_copy(other, 0, way, True).wait_recv()
-                    wy_copy(other, 1, way, False).start()
-                    wc_copy(other, -WAYS[way], False).start()
-
-    for way in (0, 1):
-        a_copy(PIECES - 1, 0, way, True).wait_recv()
-        a_copy(PIECES - 1, 1, way, False).start()
+    pass_on(3)
+    for other in (1, 3, 2):
+        for way in (0, 1):
+            wy_copy(other, 0, way, True).wait_recv()
+            wy_copy(other, 1, way, False).start()
+            wc_copy(other, -WAYS[way], False).start()
 
     @pl.loop(1, PEERS)
     def _(k):
@@ -659,6 +710,9 @@
         for offset in (-1, 0, 1, 2):
             wc_copy(other, offset, True).wait_recv()
     fetch_wo.wait()
+    fetch_base.wait()
+    fetch_last.wait()
+    fetch_gain.wait()
 
     @pl.loop(0, SIDE)
     def _(other):
@@ -668,25 +722,32 @@
         for copy in xdec_copies(k, False):
             copy.start()
 
-    @pl.loop(0, SIDE)
-    def _(chunk):
-        gather_start(x_args, chunk, 0)
+    @pl.loop(0, CHUNKS)
+    def _(number):
+        gather_start(x_args, number, 0)
 
     @pl.loop(0, PIECES)
     def _(piece):
         for level in range(4):
             gather_sent(k_args, piece, level)
 
-    gather_step(x_args, 0, 0)
-    gather_step(x_args, 0, 1)
     size = 256
 
-    @pl.loop(0, SIDE + 2)
-    def _(s):
-        x_on = s < SIDE
-        next_on = s < SIDE - 1
-        f_on = jnp.logical_and(s >= 1, s < SIDE + 1)
-        p_on = s >= 2
+    @pl.loop(0, CHUNKS + 6)
+    def _(turn):
+        s = turn - 3
+        f_on = jnp.logical_and(s >= 1, s < CHUNKS + 1)
+
+        def guarded(number, step, level, args=()):
+            @pl.when(jnp.logical_and(number >= 0, number < CHUNKS))
+            def _():
+                step(*args, number, level)
+
+        def gather(number, level):
+            guarded(number, gather_step, level, (x_args,))
+
+        def scatter(number, level):
+            guarded(number, scatter_step, level)
 
         @pl.when(s == 1)
         def _():
@@ -702,38 +763,29 @@
         def _():
             normalize(s - 1)
 
-        @pl.when(x_on)
-        def _():
-            gather_step(x_args, s, 2)
-
-        @pl.when(next_on)
-        def _():
-            gather_step(x_args, s + 1, 0)
-
-        @pl.when(p_on)
-        def _():
-            scatter_step(s - 2, 0)
+        scatter(s - 2, 0)
+        gather(s + 3, 0)
+        gather(s + 2, 1)
 
         @pl.when(f_on)
         def _():
             lift(0, size)
 
-        @pl.when(next_on)
-        def _():
-            gather_step(x_args, s + 1, 1)
-
-        @pl.when(p_on)
-        def _():
-            scatter_step(s - 2, 1)
+        scatter(s - 3, 2)
+        gather(s + 1, 2)
 
         @pl.when(f_on)
         def _():
-            for tile in range(1, ffw // size):
+            lift(1, size)
+
+        scatter(s - 2, 1)
+
+        @pl.when(f_on)
+        def _():
+            for tile in range(2, ffw // size):
                 lift(tile, size)
 
-        @pl.when(p_on)
-        def _():
-            scatter_step(s - 2, 2)
+        scatter(s - 3, 3)
 
         @pl.when(f_on)
         def _():
@@ -746,13 +798,7 @@
             def _(k):
                 fdec_copy(k, False).start()
 
-        @pl.when(x_on)
-        def _():
-            gather_step(x_args, s, 3)
-
-        @pl.when(p_on)
-        def _():
-            scatter_step(s - 2, 3)
+        gather(s, 3)
 
     @pl.loop(1, PEERS)
     def _(k):
@@ -764,9 +810,14 @@
         total = total + wide(rdec[t])
     for half in (0, 1):
         part = wide(xdec[:, mine(half)]) + total[:, half * HALF : (half + 1) * HALF]
-        out_ref[PEERS * rows : PEERS * rows + SUB, half * HALF : (half + 1) * HALF] = part.astype(
+        obuf[PEERS * rows : PEERS * rows + SUB, half * HALF : (half + 1) * HALF] = part.astype(
             jnp.bfloat16
         )
+    ending = pl.ds(PEERS * rows, SUB)
+    out_last = pltpu.make_async_copy(
+        obuf.at[ending, :], out_hbm.at[ending, :], o_sem.at[CHUNKS]
+    )
+    out_last.start()
 
     @pl.loop(1, groups)
     def _(k):
@@ -791,17 +842,22 @@
         for copy in base_copies(other, False) + tuple(xdec_copies(other, False)):
             copy.wait_send()
 
-    @pl.loop(0, SIDE)
-    def _(chunk):
+    @pl.loop(0, CHUNKS)
+    def _(number):
         for level in range(4):
-            gather_sent(x_args, chunk, level)
-            scatter_sent(chunk, level)
+            gather_sent(x_args, number, level)
+            scatter_sent(number, level)
+        out_copy(number).wait()
+
+    out_last.wait()
 
 
 def layer_call(length, request, queries, pairs, segment, dec, cache, resid, owner, gains, *weights):
     wo, w_gate, w_up, w_down = weights
     rows = queries.shape[0]
     tall = SIDE * rows
+    inner = rows // PARTS
+    high = SIDE * inner
     ffw = w_gate.shape[1]
     groups = lax.axis_size("grp")
     vmem = pl.BlockSpec(memory_space=pltpu.VMEM)
@@ -813,23 +869,27 @@
     return pl.pallas_call(
         layer_kernel,
         out_shape=jax.ShapeDtypeStruct(resid.shape, bf16),
-        in_specs=[smem, smem, vmem, vmem, vmem, vmem, hbm, vmem, vmem, vmem] + [hbm] * 4,
-        out_specs=vmem,
+        in_specs=[smem, smem, hbm, hbm, vmem, vmem, hbm, hbm, vmem] + [hbm] * 5,
+        out_specs=hbm,
         scratch_shapes=[
+            pltpu.VMEM(queries.shape, bf16),
+            pltpu.VMEM(gains.shape, jnp.float32),
+            pltpu.VMEM(resid.shape, bf16),
             pltpu.VMEM((tall + SUB, D), bf16),
             pltpu.VMEM((SIDE, D, BLOCK), bf16),
             pltpu.VMEM((SIDE, SIDE, rows, D), bf16),
             pltpu.VMEM((SIDE, SIDE, rows, D), bf16),
-            pltpu.VMEM((tall + SUB, D), bf16),
-            pltpu.VMEM((tall + SUB, ffw), bf16),
-            pltpu.VMEM((SIDE, 2, SIDE, rows, QUAD), bf16),
-            pltpu.VMEM((SIDE, 2, 2, SIDE, rows, QUAD), bf16),
-            pltpu.VMEM((SIDE, 2, SIDE, rows, HALF), bf16),
-            pltpu.VMEM((SIDE, 2, 2, SIDE, rows, HALF), bf16),
+            pltpu.VMEM((high + SUB, D), bf16),
+            pltpu.VMEM((high + SUB, ffw), bf16),
+            pltpu.VMEM((CHUNKS, 2, SIDE, inner, QUAD), bf16),
+            pltpu.VMEM((CHUNKS, 2, 2, SIDE, inner, QUAD), bf16),
+            pltpu.VMEM((CHUNKS, 2, SIDE, inner, HALF), bf16),
+            pltpu.VMEM((CHUNKS, 2, 2, SIDE, inner, HALF), bf16),
             pltpu.VMEM(w_gate.shape, bf16),
             pltpu.VMEM(w_up.shape, bf16),
             pltpu.VMEM(w_down.shape, bf16),
             pltpu.VMEM((rows, WINDOW * rows), jnp.float32),
+            pltpu.VMEM((HALF, HALF), jnp.float32),
             pltpu.VMEM((groups, H, HD), bf16),
             pltpu.VMEM((PEERS, H, HD), bf16),
             pltpu.VMEM((PEERS, H, HD), bf16),
@@ -839,7 +899,8 @@
             pltpu.VMEM((SUB, D), bf16),
             pltpu.VMEM((PEERS, SUB, BLOCK), bf16),
             pltpu.VMEM((PEERS, SUB, BLOCK), bf16),
-            dma((5,)),
+            dma((10,)),
+            dma((CHUNKS + 1,)),
             *pairs_of(PIECES, 16),
             *pairs_of(groups),
             *pairs_of(PEERS),
@@ -850,8 +911,8 @@
             *pairs_of(12),
             *pairs_of(8),
             *pairs_of(8),
-            *pairs_of(SIDE, 16),
-            *pairs_of(SIDE, 16),
+            *pairs_of(CHUNKS, 16),
+            *pairs_of(CHUNKS, 16),
             *pairs_of(PEERS),
         ],
         compiler_params=pltpu.CompilerParams(
@@ -882,9 +943,9 @@
     split = resid.reshape(PEERS, rows + 1, cols)
     natural = jnp.concatenate([split[:, :rows].reshape(PEERS * rows, cols), split[:, rows]], axis=0)
     owner = tenant[0].reshape(PEERS, rows + 1)
-    main = jnp.swapaxes(owner[:, :rows].reshape(SIDE, SIDE, rows), 0, 1).reshape(PEERS * rows)
-    owner = jnp.concatenate([main, owner[:, rows]], axis=0)
-    owner = jnp.broadcast_to(owner[:, None], (tokens, HALF))
+    main = owner[:, :rows].reshape(SIDE, CHUNKS, -1)
+    owner = jnp.concatenate([jnp.swapaxes(main, 0, 1).reshape(-1), owner[:, rows]], axis=0)
+    owner = jnp.pad(owner, (0, HALF - SUB)).reshape(1, -1)
     gains = norm_gain.reshape(-1, SIDE, SIDE, 2, HALF).transpose(0, 3, 2, 1, 4).reshape(-1, D)
     result = layer_call(
         cache_len,
@@ -892,7 +953,7 @@
         pre_q,
         pre_kv,
         pre_segment,
-        dec_q.reshape(H, HD),
+        dec_q,
         cache.reshape(2, SIDE, -1, cache.shape[2]),
         natural,
         owner,
@@ -902,7 +963,7 @@
         w_up,
         w_down,
     )
-    main = result[: PEERS * rows].reshape(SIDE, SIDE, rows, cols)
+    main = result[: PEERS * rows].reshape(CHUNKS, SIDE, -1, cols)
     main = jnp.swapaxes(main, 0, 1).reshape(PEERS, rows, cols)
     last = result[PEERS * rows :].reshape(PEERS, 1, cols)
     return jnp.concatenate([main, last], axis=1).reshape(tokens, cols)

time: 209 us -> 225 us (1.077)
  Pallas kernels: 201 us -> 218 us
    pallas_call x1, Pallas kernels: 201 us -> 218 us  [layer_call(): pl.pallas_call(layer_kernel, out_shape=jax.ShapeDtypeStruct(resid.shape,...]
where the time goes in v4:
time: 225 us
  Pallas kernels  218 us (97%)
  local copies, waits for them, and re-layouts  5.1 us (2%)
    pallas_call x1, Pallas kernels, layer_call(): pl.pallas_call(layer_kernel, out_shape=jax.ShapeDtypeStruct(resid.shape,...  218 us

profile of v4, /device:TPU:0, one launch (start us, length us, event | category | flops | bytes accessed | tf_op | source)
XLA Modules:
  0.0 225.0 jit_solution(14799652244495924403)
XLA Ops:
  0.7 1.2 reshape.37
  1.9 0.0 copy-start.1
  1.9 0.0 copy-start
  2.0 0.8 pad_maximum_fusion.1.resid_hbm
  2.8 0.0 copy-done.1
  2.8 0.1 reshape_squeeze.3
  2.9 0.1 slice.27
  3.0 0.1 copy.30
  3.1 0.1 reshape.39
  3.2 0.1 reshape.40
  3.3 0.6 reshape.41.tenant_ref
  3.9 0.0 copy-done
  3.9 0.1 reshape.42
  4.0 0.7 reshape.43.gain_hbm
  4.6 218.2 %layer.1 = bf16[1040,256]{1,0:T(8,128)(2,1)} custom-call(s32[1]{0:T(128)S(6)} %copy.35.length_ref, s32[128]{0:T(128)} %request_ref.1, bf16[64,4096]{1,0:T(8,128)(2,1)} %query_hbm.1, bf16[64,2048]{1,0:T(8,128)(2,1)} %pair_hbm.1, s32[1,1024]{1,0:T(1,128)} %segment_ref.1, bf16[1,4096]{1,0:T(2,128)(2,1)} %dec_ref.1, bf16[2,4,64,2048]{3,2,1,0:T(8,128)(2,1)} %bitcast.20, ...), custom_call_target="tpu_custom_call" | custom-call | tf_op jit(solution)/shard_map/layer/pallas_call | solution.py:869
  222.8 0.0 slice-start
  222.9 0.8 slice_bitcast_fusion
  223.6 0.3 slice-done
  224.0 1.0 reshape.47
  (11 shorter events, 0.2 us)
Async XLA Ops:
  1.9 0.9 copy-start.1
  1.9 2.0 copy-start
  222.8 1.1 slice-start

commit v5 on v4

--- a/solution.py
+++ b/solution.py
@@ -20,7 +20,7 @@
 QUAD = SIDE * HALF
 SUB = 16
 PIECES = 4
-CHUNKS = 8
+CHUNKS = 4
 PARTS = CHUNKS // SIDE
 WINDOW = 10
 CORES = 2
@@ -505,7 +505,8 @@
 
     def normalize(number):
         chunk = number // PARTS
-        tbuf[...] = owners(number * high)
+        for q in range(high // HALF):
+            tbuf[q * HALF : (q + 1) * HALF, :] = owners(number * high + q * HALF)
 
         @pl.loop(0, high // SUB)
         def _(t):
@@ -733,7 +734,7 @@
 
     size = 256
 
-    @pl.loop(0, CHUNKS + 6)
+    @pl.loop(0, CHUNKS + 8)
     def _(turn):
         s = turn - 3
         f_on = jnp.logical_and(s >= 1, s < CHUNKS + 1)
@@ -763,32 +764,28 @@
         def _():
             normalize(s - 1)
 
-        scatter(s - 2, 0)
         gather(s + 3, 0)
         gather(s + 2, 1)
+        gather(s + 1, 2)
 
         @pl.when(f_on)
         def _():
             lift(0, size)
 
-        scatter(s - 3, 2)
-        gather(s + 1, 2)
+        scatter(s - 5, 3)
+        scatter(s - 4, 2)
 
         @pl.when(f_on)
         def _():
             lift(1, size)
 
-        scatter(s - 2, 1)
+        scatter(s - 3, 1)
+        scatter(s - 2, 0)
 
         @pl.when(f_on)
         def _():
             for tile in range(2, ffw // size):
                 lift(tile, size)
-
-        scatter(s - 3, 3)
-
-        @pl.when(f_on)
-        def _():
             lower(s - 1)
             scatter_start(s - 1, 0)
 
@@ -889,7 +886,7 @@
             pltpu.VMEM(w_up.shape, bf16),
             pltpu.VMEM(w_down.shape, bf16),
             pltpu.VMEM((rows, WINDOW * rows), jnp.float32),
-            pltpu.VMEM((HALF, HALF), jnp.float32),
+            pltpu.VMEM((high, HALF), jnp.float32),
             pltpu.VMEM((groups, H, HD), bf16),
             pltpu.VMEM((PEERS, H, HD), bf16),
             pltpu.VMEM((PEERS, H, HD), bf16),

time: 225 us -> 185 us (0.82)
  Pallas kernels: 218 us -> 178 us
    pallas_call x1, Pallas kernels: 218 us -> 178 us  [layer_call(): pl.pallas_call(layer_kernel, out_shape=jax.ShapeDtypeStruct(resid.shape,...]
where the time goes in v5:
time: 185 us
  Pallas kernels  178 us (96%)
  local copies, waits for them, and re-layouts  5.06 us (3%)
    pallas_call x1, Pallas kernels, layer_call(): pl.pallas_call(layer_kernel, out_shape=jax.ShapeDtypeStruct(resid.shape,...  178 us

profile of v5, /device:TPU:0, one launch (start us, length us, event | category | flops | bytes accessed | tf_op | source)
XLA Modules:
  0.0 185.2 jit_solution(12718562457306399044)
XLA Ops:
  0.7 1.2 reshape.37
  1.9 0.0 copy-start.1
  1.9 0.0 copy-start
  2.0 0.8 pad_maximum_fusion.1.resid_hbm
  2.8 0.0 copy-done.1
  2.8 0.1 reshape_squeeze.3
  2.9 0.2 slice_reduce_fusion
  3.1 0.1 reshape.40
  3.2 0.6 reshape.41.tenant_ref
  3.8 0.0 copy-done
  3.8 0.1 reshape.42
  3.9 0.7 reshape.43.gain_hbm
  4.6 178.5 %layer.1 = bf16[1040,256]{1,0:T(8,128)(2,1)} custom-call(s32[1]{0:T(128)S(6)} %copy.38.length_ref, s32[128]{0:T(128)} %request_ref.1, bf16[64,4096]{1,0:T(8,128)(2,1)} %query_hbm.1, bf16[64,2048]{1,0:T(8,128)(2,1)} %pair_hbm.1, s32[1,1024]{1,0:T(1,128)} %segment_ref.1, bf16[1,4096]{1,0:T(2,128)(2,1)} %dec_ref.1, bf16[2,4,64,2048]{3,2,1,0:T(8,128)(2,1)} %bitcast.21, ...), custom_call_target="tpu_custom_call" | custom-call | tf_op jit(solution)/shard_map/layer/pallas_call | solution.py:866
  183.1 0.0 slice-start
  183.1 0.8 slice_bitcast_fusion
  183.9 0.3 slice-done
  184.2 1.0 reshape.47
  (11 shorter events, 0.2 us)
Async XLA Ops:
  1.9 0.9 copy-start.1
  1.9 1.9 %copy-start = (f32[4,4096]{1,0:T(4,128)S(1)}, f32[4,4096]{1,0:T(4,128)}, u32[]{:S(2)}) copy-start(f32[4,4096]{1,0:T(4,128)} %param.24) | copy-start | bytes 196612
  183.1 1.1 slice-start

commit v6 on v5

--- a/solution.py
+++ b/solution.py
@@ -49,6 +49,9 @@
     qbuf,
     gbuf,
     obuf,
+    nbuf,
+    ndec,
+    tbase,
     abuf,
     wbuf,
     xbuf,
@@ -202,9 +205,14 @@
         each(lambda half, way: gather_copy(*args, chunk, level, half, way, False).start())
 
     def gather_step(args, chunk, level):
-        each(lambda half, way: gather_copy(*args, chunk, level, half, way, True).wait_recv())
-        if level < 3:
-            gather_start(args, chunk, level + 1)
+        for half in (0, 1):
+            for way in (0, 1):
+                gather_copy(*args, chunk, level, half, way, True).wait_recv()
+                if level % 2 == 0:
+                    gather_copy(*args, chunk, level + 1, half, way, False).start()
+            if level == 1:
+                for way in (0, 1):
+                    gather_copy(*args, chunk, 2, half, way, False).start()
 
     def gather_sent(args, chunk, level):
         each(lambda half, way: gather_copy(*args, chunk, level, half, way, False).wait_send())
@@ -288,14 +296,14 @@
         last = pl.ds(PEERS * rows, PEERS)
         return (
             remote(
-                resid_hbm.at[start, :],
+                nbuf.at[start, :],
                 rbuf.at[slot, pl.ds(0, tall), :],
                 b_send.at[2 * k],
                 b_recv.at[2 * k],
                 peer,
             ),
             remote(
-                resid_hbm.at[last, :],
+                nbuf.at[last, :],
                 rbuf.at[slot, pl.ds(tall, PEERS), :],
                 b_send.at[2 * k + 1],
                 b_recv.at[2 * k + 1],
@@ -357,10 +365,12 @@
     def scatter_step(number, level):
         chunk, span = number // PARTS, within(number)
         for half in (0, 1):
-            for way in (0, 1):
-                scatter_copy(number, level, half, way).wait_recv()
+            if level % 2 == 1:
+                for way in (0, 1):
+                    scatter_copy(number, level, half, way).wait_recv()
             if level % 2 == 0:
                 for way in (0, 1):
+                    scatter_copy(number, level, half, way).wait_recv()
                     cols = (far_lanes if level == 0 else near_lanes)(half, WAYS[way])
                     some = within(number, way)
                     landed = (r1 if level == 0 else r3)[number, half, :, half_of(way), :]
@@ -500,7 +510,7 @@
             write(cols, (wide(read(cols)) * inverse * gain).astype(jnp.bfloat16))
 
     def owners(base):
-        part = tenant_ref[:, lanes(base, HALF)].astype(jnp.float32)
+        part = tbase[:, lanes(base, HALF)].astype(jnp.float32)
         return jnp.transpose(jnp.broadcast_to(part, (HALF, HALF)))
 
     def normalize(number):
@@ -534,13 +544,19 @@
 
     def lower(number):
         @pl.loop(0, D // QUAD)
-        def _(tile):
+        def _(i):
+            base = jnp.where(i % 2 == 0, z, x)
+            tile = (i % 2) * SIDE + (base + 2 - i // 2 + SIDE) % SIDE
             cols = lanes(tile * QUAD, QUAD)
             part = jnp.dot(hidden[...], wd_ref[:, cols], preferred_element_type=jnp.float32)
             part = part.astype(jnp.bfloat16)
             pbuf[number // PARTS, :, within(number), cols] = part[:high].reshape(
                 SIDE, part_rows, QUAD
             )
+
+            @pl.when(i == 1)
+            def _():
+                scatter_start(number, 0)
 
             @pl.when(number == 0)
             def _():
@@ -585,16 +601,13 @@
     def _(k):
         group_copy(k, False).start()
 
-    for piece in range(PIECES):
-        gather_start(k_args, piece, 0)
+    gather_start(k_args, 0, 0)
     for way in (0, 1):
         wz_copy(0, way, False).start()
+    for piece in range(1, PIECES):
+        gather_start(k_args, piece, 0)
     fetch_wo = local(wo_hbm, wbuf.at[z], 4)
-    fetch_gain = local(gain_hbm, gbuf, 7)
-    tall_at = pl.ds(pl.multiple_of(z * tall, tall), tall)
-    last_at = pl.ds(PEERS * rows, PEERS)
-    fetch_base = local(resid_hbm.at[tall_at, :], rbuf.at[z, pl.ds(0, tall), :], 8)
-    fetch_last = local(resid_hbm.at[last_at, :], rbuf.at[z, pl.ds(tall, PEERS), :], 9)
+    fetch_base = local(resid_hbm, obuf, 8)
     mask()
     near_order = ((0, 0), (1, 0), (0, 1), (2, 0), (1, 1), (3, 0), (2, 1), (3, 1))
     for piece, level in near_order:
@@ -617,6 +630,17 @@
 
     incoming[me] = outgoing[me]
     fetch_query.wait()
+
+    def wo_along_y(other):
+        for way in (0, 1):
+            wy_copy(other, 0, way, True).wait_recv()
+            wy_copy(other, 1, way, False).start()
+            wc_copy(other, -WAYS[way], False).start()
+
+    def wo_to_core(other):
+        for way in (0, 1):
+            wy_copy(other, 1, way, True).wait_recv()
+        wc_copy(other, 2, False).start()
 
     def attend(piece):
         gather_step(k_args, piece, 3)
@@ -649,11 +673,31 @@
     attend(1)
     pass_on(0)
     gather_step(k_args, 3, 2)
+    fetch_base.wait()
+    tbase[...] = jnp.zeros_like(tbase)
+    for t in range(PEERS):
+        for part in range(PARTS):
+            at = ((t % SIDE) * PARTS + part) * high + (t // SIDE) * part_rows
+            of = t * (rows + 1) + part * part_rows
+            tbase[:, at : at + part_rows] = tenant_ref[:, of : of + part_rows]
+        at, of = PEERS * rows + t, t * (rows + 1) + rows
+        tbase[:, at : at + 1] = tenant_ref[:, of : of + 1]
+        first_row = t * (rows + 1)
+        nbuf[t * rows : (t + 1) * rows, :] = obuf[first_row : first_row + rows, :]
+        own_row = wide(obuf[first_row + rows : first_row + rows + 1, :])
+        ndec[t : t + 1, :] = own_row
+    nbuf[PEERS * rows :, :] = ndec[...].astype(jnp.bfloat16)
+    rbuf[z, 0:tall, :] = nbuf[pl.ds(pl.multiple_of(z * tall, tall), tall), :]
+    rbuf[z, tall:, :] = nbuf[PEERS * rows :, :]
     for k in (1, 2, 3):
         for copy in base_copies(k, False):
             copy.start()
     attend(2)
     pass_on(1)
+    wo_along_y(1)
+    wo_along_y(3)
+    attend(3)
+    pass_on(2)
     fetch.wait()
 
     @pl.loop(1, PEERS)
@@ -667,8 +711,8 @@
         dec_copy(k, False).start()
 
     dbuf[me] = own[...]
-    attend(3)
-    pass_on(2)
+
+    wo_along_y(2)
 
     @pl.loop(0, PEERS)
     def _(t):
@@ -681,13 +725,11 @@
             pltpu.make_async_copy(wg_hbm.at[source, :], wg_ref.at[inside, :], w_sem.at[1]).start()
             pltpu.make_async_copy(wu_hbm.at[source, :], wu_ref.at[inside, :], w_sem.at[2]).start()
             pltpu.make_async_copy(wd_hbm.at[:, source], wd_ref.at[:, target], w_sem.at[3]).start()
+            pltpu.make_async_copy(gain_hbm.at[:, source], gbuf.at[:, inside], w_sem.at[7]).start()
 
     pass_on(3)
-    for other in (1, 3, 2):
-        for way in (0, 1):
-            wy_copy(other, 0, way, True).wait_recv()
-            wy_copy(other, 1, way, False).start()
-            wc_copy(other, -WAYS[way], False).start()
+    wo_to_core(1)
+    wo_to_core(3)
 
     @pl.loop(1, PEERS)
     def _(k):
@@ -697,27 +739,22 @@
         abuf[tall : tall + SUB, head * HD : (head + 1) * HD] = dbuf[:, head, :].astype(
             jnp.bfloat16
         )
-    for other in (1, 3, 2):
-        for way in (0, 1):
-            wy_copy(other, 1, way, True).wait_recv()
-        wc_copy(other, 2, False).start()
     for k in (1, 2, 3):
         for copy in base_copies(k, True):
             copy.wait_recv()
     for piece in range(PIECES):
         for way in (0, 1):
             a_copy(piece, 1, way, True).wait_recv()
-    for other in (1, 2, 3):
-        for offset in (-1, 0, 1, 2):
-            wc_copy(other, offset, True).wait_recv()
     fetch_wo.wait()
-    fetch_base.wait()
-    fetch_last.wait()
-    fetch_gain.wait()
-
-    @pl.loop(0, SIDE)
-    def _(other):
-        project(other)
+    pltpu.make_async_copy(gbuf, gbuf, w_sem.at[7]).wait()
+
+    for other in (0, 1, 3, 2):
+        if other > 0:
+            for offset in (-1, 0, 1, 2):
+                wc_copy(other, offset, True).wait_recv()
+        project(hop(z, other))
+        if other == 0:
+            wo_to_core(2)
 
     for k in (1, 2, 3):
         for copy in xdec_copies(k, False):
@@ -787,7 +824,6 @@
             for tile in range(2, ffw // size):
                 lift(tile, size)
             lower(s - 1)
-            scatter_start(s - 1, 0)
 
         @pl.when(s == 1)
         def _():
@@ -872,6 +908,9 @@
             pltpu.VMEM(queries.shape, bf16),
             pltpu.VMEM(gains.shape, jnp.float32),
             pltpu.VMEM(resid.shape, bf16),
+            pltpu.VMEM(resid.shape, bf16),
+            pltpu.VMEM((PEERS, BLOCK), jnp.float32),
+            pltpu.VMEM((1, resid.shape[0] + HALF - SUB), jnp.int32),
             pltpu.VMEM((tall + SUB, D), bf16),
             pltpu.VMEM((SIDE, D, BLOCK), bf16),
             pltpu.VMEM((SIDE, SIDE, rows, D), bf16),
@@ -937,13 +976,6 @@
 ):
     rows = pre_q.shape[0]
     tokens, cols = resid.shape
-    split = resid.reshape(PEERS, rows + 1, cols)
-    natural = jnp.concatenate([split[:, :rows].reshape(PEERS * rows, cols), split[:, rows]], axis=0)
-    owner = tenant[0].reshape(PEERS, rows + 1)
-    main = owner[:, :rows].reshape(SIDE, CHUNKS, -1)
-    owner = jnp.concatenate([jnp.swapaxes(main, 0, 1).reshape(-1), owner[:, rows]], axis=0)
-    owner = jnp.pad(owner, (0, HALF - SUB)).reshape(1, -1)
-    gains = norm_gain.reshape(-1, SIDE, SIDE, 2, HALF).transpose(0, 3, 2, 1, 4).reshape(-1, D)
     result = layer_call(
         cache_len,
         slot_request,
@@ -952,9 +984,9 @@
         pre_segment,
         dec_q,
         cache.reshape(2, SIDE, -1, cache.shape[2]),
-        natural,
-        owner,
-        gains,
+        resid,
+        tenant,
+        norm_gain,
         wo,
         w_gate,
         w_up,

time: 185 us -> 176 us (0.951)
  Pallas kernels: 178 us -> 172 us
  local copies, waits for them, and re-layouts: 5.06 us -> 2.79 us
    pallas_call x1, Pallas kernels: 178 us -> 172 us  [layer_call(): pl.pallas_call(layer_kernel, out_shape=jax.ShapeDtypeStruct(resid.shape,...]
    reshape x6 -> x0, local copies, waits for them, and re-layouts: 2.66 us -> none  [the longest x1 1.22 us: shards(): split = resid.reshape(PEERS, rows + 1, cols)]
where the time goes in v6:
time: 176 us
  Pallas kernels  172 us (98%)
  local copies, waits for them, and re-layouts  2.79 us (2%)
    pallas_call x1, Pallas kernels, layer_call(): pl.pallas_call(layer_kernel, out_shape=jax.ShapeDtypeStruct(resid.shape,...  172 us

profile of v6, /device:TPU:0, one launch (start us, length us, event | category | flops | bytes accessed | tf_op | source)
XLA Modules:
  0.0 175.9 jit_solution(5827325330433143564)
XLA Ops:
  0.7 172.4 %layer.1 = bf16[1040,256]{1,0:T(8,128)(2,1)} custom-call(s32[1]{0:T(128)S(6)} %copy.18.length_ref, s32[128]{0:T(128)} %request_ref.1, bf16[64,4096]{1,0:T(8,128)(2,1)} %query_hbm.1, bf16[64,2048]{1,0:T(8,128)(2,1)} %pair_hbm.1, s32[1,1024]{1,0:T(1,128)} %segment_ref.1, bf16[1,4096]{1,0:T(2,128)(2,1)} %dec_ref.1, bf16[2,4,64,2048]{3,2,1,0:T(8,128)(2,1)} %bitcast.9, ...), custom_call_target="tpu_custom_call" | custom-call | tf_op jit(solution)/shard_map/layer/pallas_call | solution.py:902
  173.0 0.7 slice_bitcast_fusion
  173.7 1.1 slice.6
  174.9 1.0 reshape.19
  (3 shorter events, 0.1 us)

commit v7 on v6

--- a/solution.py
+++ b/solution.py
@@ -358,10 +358,6 @@
     def mine(half):
         return lanes(half * WIDE + x * QUAD + z * HALF, HALF)
 
-    def out_copy(number):
-        span = pl.ds(pl.multiple_of(number * high, high), high)
-        return pltpu.make_async_copy(obuf.at[span, :], out_hbm.at[span, :], o_sem.at[number])
-
     def scatter_step(number, level):
         chunk, span = number // PARTS, within(number)
         for half in (0, 1):
@@ -399,7 +395,13 @@
                     high, HALF
                 )
         if level == 3:
-            out_copy(number).start()
+            for k in range(CHUNKS):
+                @pl.when(number == k)
+                def _():
+                    for tz in range(SIDE):
+                        at = (tz * SIDE + k // PARTS) * (rows + 1) + (k % PARTS) * part_rows
+                        of = k * high + tz * part_rows
+                        nbuf[at : at + part_rows, :] = obuf[of : of + part_rows, :]
 
     def scatter_sent(chunk, level):
         each(lambda half, way: scatter_copy(chunk, level, half, way).wait_send())
@@ -769,6 +771,9 @@
         for level in range(4):
             gather_sent(k_args, piece, level)
 
+    for k in (1, 2, 3):
+        for copy in base_copies(k, False):
+            copy.wait_send()
     size = 256
 
     @pl.loop(0, CHUNKS + 8)
@@ -846,10 +851,11 @@
         obuf[PEERS * rows : PEERS * rows + SUB, half * HALF : (half + 1) * HALF] = part.astype(
             jnp.bfloat16
         )
-    ending = pl.ds(PEERS * rows, SUB)
-    out_last = pltpu.make_async_copy(
-        obuf.at[ending, :], out_hbm.at[ending, :], o_sem.at[CHUNKS]
-    )
+    ndec[...] = wide(obuf[PEERS * rows : PEERS * rows + SUB, :])
+    for k in range(PEERS):
+        at = k * (rows + 1) + rows
+        nbuf[at : at + 1, :] = ndec[k : k + 1, :].astype(jnp.bfloat16)
+    out_last = pltpu.make_async_copy(nbuf, out_hbm, o_sem.at[0])
     out_last.start()
 
     @pl.loop(1, groups)
@@ -872,7 +878,7 @@
     for other in (1, 2, 3):
         for offset in (-1, 0, 1, 2):
             wc_copy(other, offset, False).wait_send()
-        for copy in base_copies(other, False) + tuple(xdec_copies(other, False)):
+        for copy in xdec_copies(other, False):
             copy.wait_send()
 
     @pl.loop(0, CHUNKS)
@@ -880,7 +886,6 @@
         for level in range(4):
             gather_sent(x_args, number, level)
             scatter_sent(number, level)
-        out_copy(number).wait()
 
     out_last.wait()
 
@@ -974,9 +979,7 @@
     w_up,
     w_down,
 ):
-    rows = pre_q.shape[0]
-    tokens, cols = resid.shape
-    result = layer_call(
+    return layer_call(
         cache_len,
         slot_request,
         pre_q,
@@ -992,10 +995,6 @@
         w_up,
         w_down,
     )
-    main = result[: PEERS * rows].reshape(CHUNKS, SIDE, -1, cols)
-    main = jnp.swapaxes(main, 0, 1).reshape(PEERS, rows, cols)
-    last = result[PEERS * rows :].reshape(PEERS, 1, cols)
-    return jnp.concatenate([main, last], axis=1).reshape(tokens, cols)
 
 
 def solution(mesh):

time: 176 us -> 176 us (level)
    unnamed x0 -> x1, local copies, waits for them, and re-layouts: none -> 1.87 us
where the time goes in v7:
time: 176 us; the launch traced here: 175 us
  Pallas kernels  173 us (98%)
  local copies, waits for them, and re-layouts  1.87 us (1%)
    pallas_call x1, Pallas kernels, layer_call(): pl.pallas_call(layer_kernel, out_shape=jax.ShapeDtypeStruct(resid.shape,...  173 us

profile of v7, /device:TPU:0, one launch (start us, length us, event | category | flops | bytes accessed | tf_op | source)
XLA Modules:
  0.0 175.1 jit_solution(9329390433889995547)
XLA Ops:
  0.7 172.6 %layer.1 = bf16[1040,256]{1,0:T(8,128)(2,1)} custom-call(s32[1]{0:T(128)S(6)} %copy.16.length_ref, s32[128]{0:T(128)} %request_ref.1, bf16[64,4096]{1,0:T(8,128)(2,1)} %query_hbm.1, bf16[64,2048]{1,0:T(8,128)(2,1)} %pair_hbm.1, s32[1,1024]{1,0:T(1,128)} %segment_ref.1, bf16[1,4096]{1,0:T(2,128)(2,1)} %dec_ref.1, bf16[2,4,64,2048]{3,2,1,0:T(8,128)(2,1)} %bitcast.1, ...), custom_call_target="tpu_custom_call" | custom-call | tf_op jit(solution)/shard_map/layer/pallas_call | solution.py:907
  173.2 1.9 %copy.17 = bf16[1040,256]{1,0:T(8,128)(2,1)} copy(bf16[1040,256]{1,0:T(8,128)(2,1)} %layer.1) | data formatting | bytes 1064960
